TPU v7x, 32 devices: a whole 2x2x4 slice. The times are simulated.
32 devices in a mesh: group: 4 (over y, x), slot: 8 (over z, core).
Axes of the slice: x: 2, y: 2, z: 4, core: 2. Of those that a mesh axis runs over, the one named last changes fastest.
Arguments:
- tokens: bfloat16 [4096, 2048], P(('group', 'slot')), may hold values from -6 to 6
- cotangent: bfloat16 [4096, 512], P(('group', 'slot')), may hold values from -0.59765625 to 0.59765625
- weight_halves: bfloat16 [32, 1024, 512], P(('group', 'slot')), may hold values from -0.125 to 0.125
- momentum_halves: bfloat16 [32, 1024, 512], P(('group', 'slot')), may hold values from -6 to 6
- old_map: int32 [4, 4], replicated, may hold values from 0 to 3, each once within a row
- new_map: int32 [4, 8], replicated, may hold values from 0 to 3, as said below
- row_ids: int32 [32, 128], P(('group', 'slot')), may hold values from 0 to 127
Outputs:
- projected: bfloat16 [4096, 512], P(('group', 'slot'))
Inputs may be any that keep to these rules, and one draw needn't show every extreme that they name: `old_map`: each row names each of the group's experts once. `new_map`: every expert is hosted by one to four new slots; among the experts of every owner group one is hosted by exactly four.
All inputs are finite; a program needn't handle non-finite values.
Results may differ from a plain program's by a relative error of at most 0.007.
Values may be sent and summed in bfloat16 or wider, within the bound.
No kernel may reach another device: no remote copies, remote signals or barrier semaphores. Data moves between devices by JAX's collectives and lax.ppermute only.
A program may use at most 64 MiB of HBM per device.

v0:
```python
import functools
import math

import jax
import jax.numpy as jnp
from jax import lax
from jax.experimental import pallas as pl
from jax.experimental.pallas import tpu as pltpu
from jax.sharding import PartitionSpec as P


coef_a = 3.4445
coef_b = -4.775
coef_c = 2.0315
momentum_rate = 0.95
step_scale = 0.01
gram_eps = 1e-06
contract_rows = (((0,), (0,)), ((), ()))
WIDTHS = (1, 1)
TAILS = ((0,), (1,))
MOST_PERMUTES = 4
LANES = 128
bf16 = jnp.bfloat16
f32 = jnp.float32


def shifted(shard, axis, stride, k):
    size = lax.axis_size(axis)
    return lax.ppermute(shard, axis, [(i, i ^ (k * stride)) for i in range(size)])


def swapped(shard):
    return shifted(shard, "slot", 1, 1)


def exchange(piece, axis, stride):
    size = lax.axis_size(axis)
    count = size // stride
    place = lax.axis_index(axis) // stride
    stacked = jnp.stack([piece(d) for d in range(count)])
    groups = [[first + stride * d for d in range(count)] for first in range(stride)]
    landed = lax.all_to_all(
        stacked,
        axis,
        split_axis=0,
        concat_axis=0,
        tiled=True,
        axis_index_groups=groups if stride > 1 else None,
    )
    return [lax.dynamic_index_in_dim(landed, place ^ k, 0, keepdims=False) for k in range(count)]


def pick_columns(token_block, which_half, slot_count):
    row_count, col_count = token_block.shape
    pieces_view = token_block.reshape(row_count, slot_count, 2, col_count // (2 * slot_count))
    chosen = lax.dynamic_index_in_dim(pieces_view, which_half, axis=2, keepdims=False)
    return chosen.reshape(row_count, col_count // 2)


def matmul(left, right):
    return jnp.dot(left.astype(bf16), right.astype(bf16), preferred_element_type=f32)


def tdot(left, right):
    return lax.dot_general(left, right, contract_rows, preferred_element_type=f32)


def update_matrix(gram):
    on_diagonal = lax.broadcasted_iota(jnp.int32, gram.shape, 0) == lax.broadcasted_iota(
        jnp.int32, gram.shape, 1
    )
    norm_sq = jnp.sum(jnp.where(on_diagonal, gram, 0.0), keepdims=True) + gram_eps
    first = gram * (1.0 / norm_sq)
    poly_first = coef_b * first + coef_c * matmul(first, first)
    half_way = coef_a * first + matmul(first, poly_first)
    second = coef_a * half_way + matmul(poly_first, half_way)
    poly_second = coef_b * second + coef_c * matmul(second, second)
    remainder = coef_a * (poly_first + poly_second) + matmul(poly_first, poly_second)
    return lax.rsqrt(norm_sq), remainder.astype(bf16)


def renew(weight, x0, x0_cols, factor, remainder, model_width):
    moved = coef_a * coef_a * x0_cols.astype(f32) + matmul(x0, remainder)
    scale = step_scale * math.sqrt(model_width) * factor
    return (weight.astype(f32) - scale * moved).astype(bf16)


def load_kernel(count, *refs):
    sources, targets, sems = refs[:count], refs[count : 2 * count], refs[2 * count]
    copies = [pltpu.make_async_copy(sources[i], targets[i], sems.at[i]) for i in range(count)]
    for copy in copies:
        copy.start()
    for copy in copies:
        copy.wait()


def own_place():
    slot = lax.axis_index("slot")
    return lax.axis_index("group"), lax.div(slot, 2), lax.rem(slot, 2)


def half_columns(ref, first, count, half):
    parts = []
    for j in range(count):
        start = (2 * (first + j) + half) * LANES
        parts.append(ref[:, pl.ds(pl.multiple_of(start, LANES), LANES)])
    return jnp.concatenate(parts, axis=1)


def front_kernel(own_ref, peer_ref, cot_ref, peer_cot_ref, momentum_ref, x0_ref, gram_ref):
    rows = x0_ref.shape[0]
    half = own_place()[2]
    cots = jnp.concatenate([cot_ref[...], peer_cot_ref[...]], axis=0)
    gram = None
    block = 2 * LANES
    for i in range(rows // block):
        toks = jnp.concatenate(
            [half_columns(ref, 2 * i, 2, half) for ref in (own_ref, peer_ref)], axis=0
        )
        part = slice(i * block, (i + 1) * block)
        x0 = momentum_rate * momentum_ref[part].astype(f32) + tdot(toks, cots)
        x0 = x0.astype(bf16)
        x0_ref[part] = x0
        middle = x0.shape[1] // 2
        left, right = x0[:, :middle], x0[:, middle:]
        term = (tdot(left, x0), tdot(right, right))
        gram = term if gram is None else (gram[0] + term[0], gram[1] + term[1])
    gram_ref[...] = jnp.concatenate(gram, axis=1).astype(bf16)


def stage_columns(hidden):
    unit = hidden // sum(WIDTHS)
    starts = [unit * sum(WIDTHS[:i]) for i in range(len(WIDTHS))]
    return [slice(start, start + unit * share) for start, share in zip(starts, WIDTHS)]


def renew_pieces(model_width, cols, x0_ref, weight_ref, factor, remainder, out_refs):
    group = own_place()[0]
    chunk = out_refs[0].shape[0]
    for k in range(len(out_refs)):
        rows = pl.ds(pl.multiple_of((group ^ k) * chunk, chunk), chunk)
        out_refs[k][...] = renew(
            weight_ref[rows, cols],
            x0_ref[rows, :],
            x0_ref[rows, cols],
            factor,
            remainder,
            model_width,
        )


def update_kernel(
    model_width,
    cols,
    own_ref,
    peer_ref,
    x0_ref,
    weight_ref,
    remainder_ref,
    factor_ref,
    *refs,
):
    out_refs, scratch = refs[:-7], refs[-7:]
    gram_bf, poly_bf, half_bf, second_bf, poly_ref, half_ref, second_ref = scratch
    hidden = gram_bf.shape[0]
    middle = hidden // 2
    upper = own_ref[...].astype(f32) + peer_ref[...].astype(f32)
    corners = upper[:, :middle] + upper[:, hidden:]
    on_diagonal = lax.broadcasted_iota(jnp.int32, corners.shape, 0) == lax.broadcasted_iota(
        jnp.int32, corners.shape, 1
    )
    norm_sq = jnp.sum(jnp.where(on_diagonal, corners, 0.0), keepdims=True) + gram_eps
    inverse = 1.0 / norm_sq
    lower = jnp.concatenate([upper[:, middle:hidden].T, upper[:, hidden:]], axis=1)
    grams = (upper[:, :hidden], lower)
    blocks = (slice(0, middle), slice(middle, hidden))
    for part, gram in zip(blocks, grams):
        gram_bf[part] = gram.astype(bf16)
    for part, gram in zip(blocks, grams):
        first = gram * inverse
        square = jnp.dot(gram_bf[part], gram_bf[...], preferred_element_type=f32)
        poly = coef_b * first + (coef_c * inverse * inverse) * square
        poly_ref[part] = poly
        poly_bf[part] = poly.astype(bf16)
        half = coef_a * first + inverse * jnp.dot(
            poly_bf[part], gram_bf[...], preferred_element_type=f32
        )
        half_ref[part] = half
        half_bf[part] = half.astype(bf16)
    for part in blocks:
        second = coef_a * half_ref[part] + jnp.dot(
            half_bf[part], poly_bf[...], preferred_element_type=f32
        )
        second_ref[part] = second
        second_bf[part] = second.astype(bf16)
    for part in blocks:
        square = jnp.dot(second_bf[part], second_bf[...], preferred_element_type=f32)
        poly = coef_b * second_ref[part] + coef_c * square
        crossed = jnp.dot(poly.astype(bf16), poly_bf[...], preferred_element_type=f32)
        remainder_ref[part] = (coef_a * (poly_ref[part] + poly) + crossed).astype(bf16)
    factor = lax.rsqrt(norm_sq)
    factor_ref[...] = jnp.broadcast_to(factor, factor_ref.shape)
    remainder = remainder_ref[:, cols]
    renew_pieces(model_width, cols, x0_ref, weight_ref, factor, remainder, out_refs)


def later_kernel(model_width, cols, remainder_ref, factor_ref, x0_ref, weight_ref, *out_refs):
    remainder = remainder_ref[:, cols]
    renew_pieces(model_width, cols, x0_ref, weight_ref, factor_ref[:1, :1], remainder, out_refs)


def choose_kernel(
    hosts, old_ref, new_ref, own_ref, peer_ref, ids_ref, peer_ids_ref, which_ref, *out_refs
):
    _, rows, chunk = out_refs[0].shape
    group, plane, half = own_place()
    planes = old_ref.shape[1]
    for k in range(len(out_refs)):
        for rel in range(2):
            wanted_slot = 2 * plane + (half ^ rel)
            owner = lax.div(wanted_slot, hosts)
            expert = new_ref[group ^ k, wanted_slot]
            holder = jnp.int32(0)
            for p in range(planes):
                holder = jnp.where(old_ref[owner, p] == expert, p, holder)
            which_ref[2 * k + rel] = plane ^ holder
    for rel, (ref, ids) in enumerate(((own_ref, ids_ref), (peer_ref, peer_ids_ref))):
        place = lax.broadcasted_iota(jnp.int32, (rows, rows), 0)
        pick = jnp.where(place == ids[...], 1.0, 0.0).astype(bf16)
        for k, out in enumerate(out_refs):
            count = chunk // LANES
            cols = half_columns(ref, (group ^ k) * count, count, half)
            out[rel] = tdot(pick, cols).astype(bf16)


def route_kernel(count, *refs):
    ins, outs, store = refs[:count], refs[count : 2 * count], refs[2 * count]
    group, plane, _ = own_place()
    for k in range(count):
        store[k] = ins[k][...]
    for k in range(count):
        outs[k][...] = store[group ^ plane ^ k]


def project_kernel(count, planes, stages, which_ref, *refs):
    toks, weights = refs[:count], refs[count : count + planes * stages]
    keep_ref, send_ref = refs[count + planes * stages :][:2]
    stores = refs[count + planes * stages + 2 :]
    for stage in range(stages):
        for k in range(planes):
            stores[stage][k] = weights[stage * planes + k][...]
    for rel in (1, 0):
        for k in range(count):
            place = which_ref[2 * k + rel]
            start = 0
            for store in stores:
                cols = slice(start, start + store.shape[2])
                start = cols.stop
                got = jnp.dot(toks[k][rel], store[place], preferred_element_type=f32)
                if rel == 0:
                    keep_ref[k, :, cols] = got
                else:
                    send_ref[k, :, cols] = got.astype(bf16)


def join_kernel(count, keep_ref, other_ref, *out_refs):
    for k in range(count):
        out_refs[k][...] = (keep_ref[k] + other_ref[k].astype(f32)).astype(bf16)


def finish_kernel(count, *refs):
    out_ref = refs[-1]
    start = 0
    for tail in range(len(TAILS)):
        mine = refs[tail * count : (tail + 1) * count]
        cols = slice(start, start + mine[0].shape[1])
        start = cols.stop
        out_ref[:, cols] = sum(r[...].astype(f32) for r in mine).astype(out_ref.dtype)


VMEM, SMEM, HBM = pltpu.VMEM, pltpu.SMEM, pltpu.HBM


def call(kernel, arrays, outs, scratch=(), spaces=None, out_spaces=None):
    spaces = spaces or [VMEM] * len(arrays)
    out_spaces = out_spaces or [VMEM] * len(outs)
    made = {
        VMEM: lambda shape, dtype: pltpu.VMEM(shape, dtype),
        SMEM: lambda shape, dtype: pltpu.SMEM(shape, dtype),
        None: jax.ShapeDtypeStruct,
    }
    return pl.pallas_call(
        kernel,
        out_shape=[made[where](*out) for where, out in zip(out_spaces, outs)],
        in_specs=[pl.BlockSpec(memory_space=where or SMEM) for where in spaces],
        out_specs=[pl.BlockSpec(memory_space=where or VMEM) for where in out_spaces],
        scratch_shapes=list(scratch),
        compiler_params=pltpu.CompilerParams(vmem_limit_bytes=16 * 2**20),
    )(
        *[
            a if where is None else pltpu.with_memory_space_constraint(a, where)
            for where, a in zip(spaces, arrays)
        ]
    )


def on_device(tokens, cotangent, weight_halves, momentum_halves, old_map, new_map, row_ids):
    slot_count = lax.axis_size("slot")
    group_count = lax.axis_size("group")
    planes = slot_count // 2
    inputs = (
        tokens,
        cotangent,
        weight_halves[0],
        momentum_halves[0],
        old_map,
        new_map,
        row_ids,
    )
    fits = group_count == planes and planes <= MOST_PERMUTES
    if fits and tokens.shape[1] == 2 * slot_count * LANES:
        return by_permutes(*inputs)
    return by_all_to_all(*inputs)


FIRST = (3, 2, 1)
ACROSS = (3, 2, 1)


def spread(mine, axis, stride, order):
    landed = [mine[0]] + [None] * (len(mine) - 1)
    for k in order:
        if k < len(mine):
            landed[k] = shifted(mine[k], axis, stride, k)
    return landed


def by_permutes(tokens, cotangent, weight, momentum, old_map, new_map, row_ids):
    slot_count = lax.axis_size("slot")
    count = lax.axis_size("group")
    planes = slot_count // 2
    hosts = slot_count // count
    row_count, model_width = tokens.shape
    hidden = cotangent.shape[1]
    half_rows = model_width // 2
    chunk = half_rows // count
    columns = stage_columns(hidden)

    peer_tokens = swapped(tokens)
    peer_cot = swapped(cotangent)

    def loaded(*arrays):
        return call(
            functools.partial(load_kernel, len(arrays)),
            arrays,
            [(a.shape, a.dtype) for a in arrays],
            [pltpu.SemaphoreType.DMA((len(arrays),))],
            spaces=[HBM] * len(arrays),
        )

    tokens_in, cot_in, momentum_in = loaded(tokens, cotangent, momentum)
    x0, own_gram = call(
        front_kernel,
        [tokens_in, peer_tokens, cot_in, peer_cot, momentum_in],
        [((half_rows, hidden), bf16), ((hidden // 2, hidden + hidden // 2), bf16)],
    )
    peer_gram = swapped(own_gram)
    weight_in, ids_in = loaded(weight, row_ids)
    peer_ids = swapped(row_ids)

    which, *token_cuts = call(
        functools.partial(choose_kernel, hosts),
        [old_map, new_map, tokens_in, peer_tokens, ids_in, peer_ids],
        [((2 * count,), jnp.int32)] + [((2, row_count, chunk), bf16)] * count,
        spaces=[None, None] + [VMEM] * 4,
        out_spaces=[SMEM] + [VMEM] * count,
    )

    arrived = []
    for stage, cols in enumerate(columns):
        width = cols.stop - cols.start
        if stage == 0:
            remainder, factor, *pieces = call(
                functools.partial(update_kernel, model_width, cols),
                [own_gram, peer_gram, x0, weight_in],
                [((hidden, hidden), bf16), ((8, LANES), f32)] + [((chunk, width), bf16)] * count,
                [pltpu.VMEM((hidden, hidden), bf16)] * 4
                + [pltpu.VMEM((hidden, hidden), f32)] * 3,
            )
        else:
            pieces = call(
                functools.partial(later_kernel, model_width, cols),
                [remainder, factor, x0, weight_in],
                [((chunk, width), bf16)] * count,
            )
        landed = spread(pieces, "group", 1, FIRST)
        routed = call(
            functools.partial(route_kernel, count),
            landed,
            [((chunk, width), bf16)] * count,
            [pltpu.VMEM((count, chunk, width), bf16)],
        )
        arrived.append(spread(routed, "slot", 2, ACROSS))

    requested = spread(token_cuts, "group", 1, FIRST)

    returned = []
    for stages in TAILS:
        widths = [columns[i].stop - columns[i].start for i in stages]
        keep, send = call(
            functools.partial(project_kernel, count, planes, len(stages)),
            [which] + requested + sum((arrived[i] for i in stages), []),
            [((count, row_count, sum(widths)), f32), ((count, row_count, sum(widths)), bf16)],
            [pltpu.VMEM((planes, chunk, width), bf16) for width in widths],
            spaces=[SMEM] + [VMEM] * (count + planes * len(stages)),
        )
        other = swapped(send)
        mine = call(
            functools.partial(join_kernel, count),
            [keep, other],
            [((row_count, sum(widths)), bf16)] * count,
        )
        returned += spread(mine, "group", 1, FIRST)
    return call(
        functools.partial(finish_kernel, count),
        returned,
        [((row_count, hidden), bf16)],
        out_spaces=[None],
    )[0]


def by_all_to_all(tokens, cotangent, weight, momentum, old_map, new_map, row_ids):
    slot_count = lax.axis_size("slot")
    group_count = lax.axis_size("group")
    planes = slot_count // 2
    owners = max(1, 2 * group_count // slot_count)
    row_count, model_width = tokens.shape
    hidden = cotangent.shape[1]
    half_rows = model_width // 2
    chunk = half_rows // group_count
    half = lax.axis_index("slot") % 2
    plane = lax.axis_index("slot") // 2
    group = lax.axis_index("group")
    hosts = slot_count // group_count

    from_group = group ^ jnp.arange(group_count)
    wanted_slot = 2 * plane + (half ^ jnp.arange(2))
    experts = new_map[from_group[:, None], wanted_slot[None, :]]
    lists = old_map[wanted_slot // hosts]
    holder = jnp.argmax((lists[None] == experts[:, :, None]).astype(jnp.int32), axis=2)

    peer_cot = swapped(cotangent)
    peer_tokens = swapped(pick_columns(tokens, 1 - half, slot_count))
    own_tokens = pick_columns(tokens, half, slot_count)
    gradient = tdot(own_tokens, cotangent) + tdot(peer_tokens, peer_cot)
    x0 = (momentum_rate * momentum.astype(f32) + gradient).astype(bf16)
    own_gram = tdot(x0, x0).astype(bf16)
    factor, remainder = update_matrix(own_gram.astype(f32) + swapped(own_gram).astype(f32))
    renewed = renew(weight, x0, x0, factor, remainder, model_width)

    pick = (row_ids[0][:, None] == jnp.arange(row_count)[None, :]).astype(bf16)
    chosen = jnp.dot(pick, tokens, preferred_element_type=f32).astype(bf16)
    own_chosen = pick_columns(chosen, half, slot_count)
    peer_chosen = swapped(pick_columns(chosen, 1 - half, slot_count))
    both = jnp.stack([own_chosen, peer_chosen]).reshape(2, row_count, group_count, chunk)
    requested = jnp.stack(exchange(lambda d: both[:, :, d], "group", 1))
    outputs = []
    for cols in (slice(0, hidden // 2), slice(hidden // 2, hidden)):
        width = cols.stop - cols.start
        chunks = renewed[:, cols].reshape(group_count, chunk, width)
        in_plane = jnp.stack(exchange(lambda d: chunks[d], "group", 1))
        by_owner = jnp.take(in_plane, group ^ jnp.arange(group_count), axis=0)
        by_plane = by_owner.reshape(planes, owners, chunk, width)
        arrived = jnp.stack(exchange(lambda d: by_plane[d], "slot", 2))
        partial = [
            jnp.einsum(
                "ktc,kcw->ktw",
                requested[:, rel],
                arrived[plane ^ holder[:, rel], (half ^ rel) * owners // 2],
                preferred_element_type=f32,
            )
            for rel in range(2)
        ]
        other = swapped(partial[1].astype(bf16))
        summed = (partial[0] + other.astype(f32)).astype(bf16)
        by_group = jnp.take(summed, group ^ jnp.arange(group_count), axis=0)
        returned = exchange(lambda d: by_group[d], "group", 1)
        outputs.append(sum(r.astype(f32) for r in returned).astype(bf16))
    return jnp.concatenate(outputs, axis=1)


def solution(mesh):
    placed = (
        P(("group", "slot"), None),
        P(("group", "slot"), None),
        P(("group", "slot"), None, None),
        P(("group", "slot"), None, None),
        P(),
        P(),
        P(("group", "slot"), None),
    )
    return jax.shard_map(
        on_device, mesh=mesh, in_specs=placed, out_specs=P(("group", "slot"), None), check_vma=False
    )
```

profile of v0, /device:TPU:0, one launch (start us, length us, event | category | flops | bytes accessed | tf_op | source)
XLA Modules:
  0.0 62.6 jit_solution(2051248678259446715)
XLA Ops:
  0.0 0.5 collective-permute-start
  0.5 0.0 collective-permute-start.5
  0.5 1.5 %shard_map.73 = (bf16[128,2048]{1,0:T(8,128)(2,1)S(1)}, bf16[128,512]{1,0:T(8,128)(2,1)S(1)}, bf16[1024,512]{1,0:T(8,128)(2,1)S(1)}) custom-call(bf16[128,2048]{1,0:T(8,128)(2,1)} %refs_0_.1, bf16[128,512]{1,0:T(8,128)(2,1)} %refs_1_.2, bf16[1024,512]{1,0:T(8,128)(2,1)} %bitcast.3), custom_call_target="tpu_custom_call" | custom-call | tf_op jit(solution)/shard_map/pallas_call | solution.py:292
  2.0 0.5 collective-permute-done.5.peer_cot_ref
  2.4 0.0 collective-permute-done.peer_ref
  2.4 1.4 %shard_map.76 = (bf16[1024,512]{1,0:T(8,128)(2,1)S(1)}, bf16[256,768]{1,0:T(8,128)(2,1)S(1)}) custom-call(bf16[128,2048]{1,0:T(8,128)(2,1)S(1)} %get-tuple-element.47.own_ref, bf16[128,2048]{1,0:T(8,128)(2,1)S(1)} %collective-permute-done.peer_ref, bf16[128,512]{1,0:T(8,128)(2,1)S(1)} %get-tuple-element.54.cot_ref, ...), custom_call_target="tpu_custom_call" | custom-call | tf_op jit(solution)/shard_map/pallas_call | solution.py:292
  3.8 0.4 collective-permute-start.6
  4.2 1.2 %shard_map.74 = (bf16[1024,512]{1,0:T(8,128)(2,1)S(1)}, s32[1,128]{1,0:T(1,128)S(1)}) custom-call(bf16[1024,512]{1,0:T(8,128)(2,1)} %bitcast.2, s32[1,128]{1,0:T(1,128)} %refs_1_.3), custom_call_target="tpu_custom_call" | custom-call | tf_op jit(solution)/shard_map/pallas_call | solution.py:292
  5.5 0.1 collective-permute-done.6.peer_ref
  5.6 2.4 %shard_map.77 = (bf16[512,512]{1,0:T(8,128)(2,1)S(1)}, f32[8,128]{1,0:T(8,128)S(1)}, bf16[256,256]{1,0:T(8,128)(2,1)S(1)}, bf16[256,256]{1,0:T(8,128)(2,1)S(1)},...) custom-call(bf16[256,768]{1,0:T(8,128)(2,1)S(1)} %get-tuple-element.56.own_ref, ...), custom_call_target="tpu_custom_call" | custom-call | tf_op jit(solution)/shard_map/pallas_call | solution.py:292
  8.0 0.5 shard_map.81
  8.5 0.0 copy-start.2
  8.5 2.9 %collective-permute-start.17 = (bf16[256,256]{1,0:T(8,128)(2,1)S(1)}, bf16[256,256]{1,0:T(8,128)(2,1)S(1)}, u32[]{:S(2)}, u32[]{:S(2)}) collective-permute-start(bf16[256,256]{1,0:T(8,128)(2,1)S(1)} %get-tuple-element.76), channel_id=1, source_target_pairs={{0,8},{8,0},{16,24},{24,16},{1,9},{9,1},{17,25},{25,17},{2,10},{10... | collective-permute-start | bytes 393224 | tf_op jit(solution)/shard_map/ppermute | solution.py:29
  11.5 1.5 %collective-permute-start.18 = (bf16[256,256]{1,0:T(8,128)(2,1)S(1)}, bf16[256,256]{1,0:T(8,128)(2,1)S(1)}, u32[]{:S(2)}, u32[]{:S(2)}) collective-permute-start(bf16[256,256]{1,0:T(8,128)(2,1)S(1)} %get-tuple-element.77), channel_id=1, source_target_pairs={{0,16},{8,24},{16,0},{24,8},{1,17},{9,25},{17,1},{25,9},{2,18},{10... | collective-permute-start | bytes 393224 | tf_op jit(solution)/shard_map/ppermute | solution.py:29
  13.0 0.0 collective-permute-start.1
  13.0 0.1 collective-permute-start.19
  13.1 1.0 %collective-permute-done.1.peer_ids_ref = s32[1,128]{1,0:T(1,128)S(1)} collective-permute-done((s32[1,128]{1,0:T(1,128)S(1)}, s32[1,128]{1,0:T(1,128)S(1)}, u32[]{:S(2)}, u32[]{:S(2)}) %collective-permute-start.1) | collective-permute-done | bytes 544 | tf_op jit(solution)/shard_map/ppermute | solution.py:29
  14.1 0.9 %shard_map.75 = (s32[8]{0:T(128)S(4)}, bf16[2,128,256]{2,1,0:T(8,128)(2,1)S(1)}, bf16[2,128,256]{2,1,0:T(8,128)(2,1)S(1)}, bf16[2,128,256]{2,1,0:T(8,128)(2,1)S(1)}, bf16[2,128,256]{2,1,0:T(8,128)(2,1)S(1)}) custom-call(s32[4,4]{1,0:T(4,128)S(1)} %copy-done, s32[4,8]{1,0:T(4,128)S(1)} %copy-done.1, bf16[128,2048]{1,0:T(8,128)(2,1)S(1)} %get-tuple-element.47.own_ref, ...), custom_call_target="tpu_custom_call" | custom-call | tf_op jit(solution)/shard_map/pallas_call | solution.py:292
  15.1 0.9 %collective-permute-start.2 = (bf16[2,128,256]{2,1,0:T(8,128)(2,1)S(1)}, bf16[2,128,256]{2,1,0:T(8,128)(2,1)S(1)}, u32[]{:S(2)}, u32[]{:S(2)}) collective-permute-start(bf16[2,128,256]{2,1,0:T(8,128)(2,1)S(1)} %get-tuple-element.51), channel_id=1, source_target_pairs={{0,8},{8,0},{16,24},{24,16},{1,9},{9,1},{17,25},{25,17},{2,10},{10... | collective-permute-start | bytes 393224 | tf_op jit(solution)/shard_map/ppermute | solution.py:29
  16.0 1.2 %collective-permute-start.7 = (bf16[256,256]{1,0:T(8,128)(2,1)S(1)}, bf16[256,256]{1,0:T(8,128)(2,1)S(1)}, u32[]{:S(2)}, u32[]{:S(2)}) collective-permute-start(bf16[256,256]{1,0:T(8,128)(2,1)S(1)} %get-tuple-element.60), channel_id=1, source_target_pairs={{0,8},{8,0},{16,24},{24,16},{1,9},{9,1},{17,25},{25,17},{2,10},{10... | collective-permute-start | bytes 393224 | tf_op jit(solution)/shard_map/ppermute | solution.py:29
  17.2 0.0 collective-permute-done.17.refs_1_
  17.2 0.9 %collective-permute-start.8 = (bf16[256,256]{1,0:T(8,128)(2,1)S(1)}, bf16[256,256]{1,0:T(8,128)(2,1)S(1)}, u32[]{:S(2)}, u32[]{:S(2)}) collective-permute-start(bf16[256,256]{1,0:T(8,128)(2,1)S(1)} %get-tuple-element.61), channel_id=1, source_target_pairs={{0,16},{8,24},{16,0},{24,8},{1,17},{9,25},{17,1},{25,9},{2,18},{10... | collective-permute-start | bytes 393224 | tf_op jit(solution)/shard_map/ppermute | solution.py:29
  18.0 0.8 %collective-permute-done.18.refs_2_ = bf16[256,256]{1,0:T(8,128)(2,1)S(1)} collective-permute-done((bf16[256,256]{1,0:T(8,128)(2,1)S(1)}, bf16[256,256]{1,0:T(8,128)(2,1)S(1)}, u32[]{:S(2)}, u32[]{:S(2)}) %collective-permute-start.18) | collective-permute-done | bytes 131104 | tf_op jit(solution)/shard_map/ppermute | solution.py:29
  18.9 1.7 %collective-permute-start.9 = (bf16[256,256]{1,0:T(8,128)(2,1)S(1)}, bf16[256,256]{1,0:T(8,128)(2,1)S(1)}, u32[]{:S(2)}, u32[]{:S(2)}) collective-permute-start(bf16[256,256]{1,0:T(8,128)(2,1)S(1)} %get-tuple-element.62), channel_id=1, source_target_pairs={{0,24},{8,16},{16,8},{24,0},{1,25},{9,17},{17,9},{25,1},{2,26},{10... | collective-permute-start | bytes 393224 | tf_op jit(solution)/shard_map/ppermute | solution.py:29
  20.6 0.0 collective-permute-done.19.refs_3_
  20.6 0.9 %collective-permute-start.3 = (bf16[2,128,256]{2,1,0:T(8,128)(2,1)S(1)}, bf16[2,128,256]{2,1,0:T(8,128)(2,1)S(1)}, u32[]{:S(2)}, u32[]{:S(2)}) collective-permute-start(bf16[2,128,256]{2,1,0:T(8,128)(2,1)S(1)} %get-tuple-element.52), channel_id=1, source_target_pairs={{0,16},{8,24},{16,0},{24,8},{1,17},{9,25},{17,1},{25,9},{2,18},{10... | collective-permute-start | bytes 393224 | tf_op jit(solution)/shard_map/ppermute | solution.py:29
  21.5 0.1 shard_map.82
  21.6 0.6 collective-permute-done.2.refs_1_
  22.2 2.4 %collective-permute-start.4 = (bf16[2,128,256]{2,1,0:T(8,128)(2,1)S(1)}, bf16[2,128,256]{2,1,0:T(8,128)(2,1)S(1)}, u32[]{:S(2)}, u32[]{:S(2)}) collective-permute-start(bf16[2,128,256]{2,1,0:T(8,128)(2,1)S(1)} %get-tuple-element.53), channel_id=1, source_target_pairs={{0,24},{8,16},{16,8},{24,0},{1,25},{9,17},{17,9},{25,1},{2,26},{10... | collective-permute-start | bytes 393224 | tf_op jit(solution)/shard_map/ppermute | solution.py:29
  24.6 0.4 collective-permute-done.7.refs_1_
  25.0 1.6 %collective-permute-start.20 = (bf16[256,256]{1,0:T(8,128)(2,1)S(1)}, bf16[256,256]{1,0:T(8,128)(2,1)S(1)}, u32[]{:S(2)}, u32[]{:S(2)}) collective-permute-start(bf16[256,256]{1,0:T(8,128)(2,1)S(1)} %get-tuple-element.80), channel_id=1, source_target_pairs={{0,2},{1,3},{2,0},{3,1},{4,6},{5,7},{6,4},{7,5},{8,10},{9,11},{10,... | collective-permute-start | bytes 393224 | tf_op jit(solution)/shard_map/ppermute | solution.py:29
  26.5 0.0 collective-permute-done.8.refs_2_
  26.5 2.6 %collective-permute-start.21 = (bf16[256,256]{1,0:T(8,128)(2,1)S(1)}, bf16[256,256]{1,0:T(8,128)(2,1)S(1)}, u32[]{:S(2)}, u32[]{:S(2)}) collective-permute-start(bf16[256,256]{1,0:T(8,128)(2,1)S(1)} %get-tuple-element.81), channel_id=1, source_target_pairs={{0,4},{1,5},{2,6},{3,7},{4,0},{5,1},{6,2},{7,3},{8,12},{9,13},{10,... | collective-permute-start | bytes 393224 | tf_op jit(solution)/shard_map/ppermute | solution.py:29
  29.1 0.0 collective-permute-done.9.refs_3_
  29.1 3.3 %collective-permute-start.22 = (bf16[256,256]{1,0:T(8,128)(2,1)S(1)}, bf16[256,256]{1,0:T(8,128)(2,1)S(1)}, u32[]{:S(2)}, u32[]{:S(2)}) collective-permute-start(bf16[256,256]{1,0:T(8,128)(2,1)S(1)} %get-tuple-element.82), channel_id=1, source_target_pairs={{0,6},{1,7},{2,4},{3,5},{4,2},{5,3},{6,0},{7,1},{8,14},{9,15},{10,... | collective-permute-start | bytes 393224 | tf_op jit(solution)/shard_map/ppermute | solution.py:29
  32.4 0.1 shard_map.78
  32.4 0.0 collective-permute-done.3.refs_2_
  32.5 0.5 collective-permute-start.10
  33.0 0.0 collective-permute-done.4.refs_3_
  33.0 2.6 %collective-permute-start.11 = (bf16[256,256]{1,0:T(8,128)(2,1)S(1)}, bf16[256,256]{1,0:T(8,128)(2,1)S(1)}, u32[]{:S(2)}, u32[]{:S(2)}) collective-permute-start(bf16[256,256]{1,0:T(8,128)(2,1)S(1)} %get-tuple-element.65), channel_id=1, source_target_pairs={{0,4},{1,5},{2,6},{3,7},{4,0},{5,1},{6,2},{7,3},{8,12},{9,13},{10,... | collective-permute-start | bytes 393224 | tf_op jit(solution)/shard_map/ppermute | solution.py:29
  35.6 1.3 %collective-permute-start.12 = (bf16[256,256]{1,0:T(8,128)(2,1)S(1)}, bf16[256,256]{1,0:T(8,128)(2,1)S(1)}, u32[]{:S(2)}, u32[]{:S(2)}) collective-permute-start(bf16[256,256]{1,0:T(8,128)(2,1)S(1)} %get-tuple-element.66), channel_id=1, source_target_pairs={{0,6},{1,7},{2,4},{3,5},{4,2},{5,3},{6,0},{7,1},{8,14},{9,15},{10,... | collective-permute-start | bytes 393224 | tf_op jit(solution)/shard_map/ppermute | solution.py:29
  36.9 1.2 %collective-permute-done.21.refs_6_ = bf16[256,256]{1,0:T(8,128)(2,1)S(1)} collective-permute-done((bf16[256,256]{1,0:T(8,128)(2,1)S(1)}, bf16[256,256]{1,0:T(8,128)(2,1)S(1)}, u32[]{:S(2)}, u32[]{:S(2)}) %collective-permute-start.21) | collective-permute-done | bytes 131104 | tf_op jit(solution)/shard_map/ppermute | solution.py:29
  38.1 0.8 %collective-permute-done.22.refs_7_ = bf16[256,256]{1,0:T(8,128)(2,1)S(1)} collective-permute-done((bf16[256,256]{1,0:T(8,128)(2,1)S(1)}, bf16[256,256]{1,0:T(8,128)(2,1)S(1)}, u32[]{:S(2)}, u32[]{:S(2)}) %collective-permute-start.22) | collective-permute-done | bytes 131104 | tf_op jit(solution)/shard_map/ppermute | solution.py:29
  39.0 0.3 shard_map.83
  39.3 0.1 collective-permute-start.23
  39.4 0.2 collective-permute-done.10.refs_5_
  39.6 10.2 %collective-permute-done.11.refs_6_ = bf16[256,256]{1,0:T(8,128)(2,1)S(1)} collective-permute-done((bf16[256,256]{1,0:T(8,128)(2,1)S(1)}, bf16[256,256]{1,0:T(8,128)(2,1)S(1)}, u32[]{:S(2)}, u32[]{:S(2)}) %collective-permute-start.11) | collective-permute-done | bytes 131104 | tf_op jit(solution)/shard_map/ppermute | solution.py:29
  49.8 0.0 collective-permute-done.12.refs_7_
  49.8 0.3 shard_map.79
  50.1 0.1 collective-permute-start.13
  50.2 0.0 collective-permute-done.23.other_ref
  50.3 1.0 %collective-permute-start.24 = (bf16[128,256]{1,0:T(8,128)(2,1)S(1)}, bf16[128,256]{1,0:T(8,128)(2,1)S(1)}, u32[]{:S(2)}, u32[]{:S(2)}) collective-permute-start(bf16[128,256]{1,0:T(8,128)(2,1)S(1)} %get-tuple-element.86), channel_id=1, source_target_pairs={{0,8},{8,0},{16,24},{24,16},{1,9},{9,1},{17,25},{25,17},{2,10},{10... | collective-permute-start | bytes 196616 | tf_op jit(solution)/shard_map/ppermute | solution.py:29
  51.3 1.8 %collective-permute-start.25 = (bf16[128,256]{1,0:T(8,128)(2,1)S(1)}, bf16[128,256]{1,0:T(8,128)(2,1)S(1)}, u32[]{:S(2)}, u32[]{:S(2)}) collective-permute-start(bf16[128,256]{1,0:T(8,128)(2,1)S(1)} %get-tuple-element.87), channel_id=1, source_target_pairs={{0,16},{8,24},{16,0},{24,8},{1,17},{9,25},{17,1},{25,9},{2,18},{10... | collective-permute-start | bytes 196616 | tf_op jit(solution)/shard_map/ppermute | solution.py:29
  53.1 0.8 %collective-permute-start.26 = (bf16[128,256]{1,0:T(8,128)(2,1)S(1)}, bf16[128,256]{1,0:T(8,128)(2,1)S(1)}, u32[]{:S(2)}, u32[]{:S(2)}) collective-permute-start(bf16[128,256]{1,0:T(8,128)(2,1)S(1)} %get-tuple-element.88), channel_id=1, source_target_pairs={{0,24},{8,16},{16,8},{24,0},{1,25},{9,17},{17,9},{25,1},{2,26},{10... | collective-permute-start | bytes 196616 | tf_op jit(solution)/shard_map/ppermute | solution.py:29
  53.8 0.0 collective-permute-done.13.other_ref
  53.9 1.0 %collective-permute-start.14 = (bf16[128,256]{1,0:T(8,128)(2,1)S(1)}, bf16[128,256]{1,0:T(8,128)(2,1)S(1)}, u32[]{:S(2)}, u32[]{:S(2)}) collective-permute-start(bf16[128,256]{1,0:T(8,128)(2,1)S(1)} %get-tuple-element.70), channel_id=1, source_target_pairs={{0,8},{8,0},{16,24},{24,16},{1,9},{9,1},{17,25},{25,17},{2,10},{10... | collective-permute-start | bytes 196616 | tf_op jit(solution)/shard_map/ppermute | solution.py:29
  54.9 1.8 %collective-permute-start.15 = (bf16[128,256]{1,0:T(8,128)(2,1)S(1)}, bf16[128,256]{1,0:T(8,128)(2,1)S(1)}, u32[]{:S(2)}, u32[]{:S(2)}) collective-permute-start(bf16[128,256]{1,0:T(8,128)(2,1)S(1)} %get-tuple-element.71), channel_id=1, source_target_pairs={{0,16},{8,24},{16,0},{24,8},{1,17},{9,25},{17,1},{25,9},{2,18},{10... | collective-permute-start | bytes 196616 | tf_op jit(solution)/shard_map/ppermute | solution.py:29
  56.7 0.0 collective-permute-done.24.refs_5_
  56.7 0.8 %collective-permute-start.16 = (bf16[128,256]{1,0:T(8,128)(2,1)S(1)}, bf16[128,256]{1,0:T(8,128)(2,1)S(1)}, u32[]{:S(2)}, u32[]{:S(2)}) collective-permute-start(bf16[128,256]{1,0:T(8,128)(2,1)S(1)} %get-tuple-element.72), channel_id=1, source_target_pairs={{0,24},{8,16},{16,8},{24,0},{1,25},{9,17},{17,9},{25,1},{2,26},{10... | collective-permute-start | bytes 196616 | tf_op jit(solution)/shard_map/ppermute | solution.py:29
  57.4 0.0 collective-permute-done.25.refs_6_
  57.4 1.3 %collective-permute-done.26.refs_7_ = bf16[128,256]{1,0:T(8,128)(2,1)S(1)} collective-permute-done((bf16[128,256]{1,0:T(8,128)(2,1)S(1)}, bf16[128,256]{1,0:T(8,128)(2,1)S(1)}, u32[]{:S(2)}, u32[]{:S(2)}) %collective-permute-start.26) | collective-permute-done | bytes 65568 | tf_op jit(solution)/shard_map/ppermute | solution.py:29
  58.8 0.8 %collective-permute-done.15.refs_2_ = bf16[128,256]{1,0:T(8,128)(2,1)S(1)} collective-permute-done((bf16[128,256]{1,0:T(8,128)(2,1)S(1)}, bf16[128,256]{1,0:T(8,128)(2,1)S(1)}, u32[]{:S(2)}, u32[]{:S(2)}) %collective-permute-start.15) | collective-permute-done | bytes 65568 | tf_op jit(solution)/shard_map/ppermute | solution.py:29
  59.5 2.3 %collective-permute-done.16.refs_3_ = bf16[128,256]{1,0:T(8,128)(2,1)S(1)} collective-permute-done((bf16[128,256]{1,0:T(8,128)(2,1)S(1)}, bf16[128,256]{1,0:T(8,128)(2,1)S(1)}, u32[]{:S(2)}, u32[]{:S(2)}) %collective-permute-start.16) | collective-permute-done | bytes 65568 | tf_op jit(solution)/shard_map/ppermute | solution.py:29
  61.8 0.7 %shard_map.85 = bf16[128,512]{1,0:T(8,128)(2,1)} custom-call(bf16[128,256]{1,0:T(8,128)(2,1)S(1)} %get-tuple-element.69.refs_0_, bf16[128,256]{1,0:T(8,128)(2,1)S(1)} %collective-permute-done.14.refs_1_, bf16[128,256]{1,0:T(8,128)(2,1)S(1)} %collective-permute-done.15.refs_2_, bf16[128,256]{1,0:T(8,128)(2,1)S(1)} %collective-permute-done.16.refs_3_, ...), custom_call_target="tpu_custom_call" | custom-call | tf_op jit(solution)/shard_map/pallas_call | solution.py:292
  (9 shorter events, 0.1 us)
Async XLA Ops:
  0.0 2.4 %collective-permute-start = (bf16[128,2048]{1,0:T(8,128)(2,1)}, bf16[128,2048]{1,0:T(8,128)(2,1)S(1)}, u32[]{:S(2)}, u32[]{:S(2)}) collective-permute-start(bf16[128,2048]{1,0:T(8,128)(2,1)} %refs_0_.1), channel_id=1, source_target_pairs={{0,1},{1,0},{2,3},{3,2},{4,5},{5,4},{6,7},{7,6},{8,9},{9,8},{10,11... | collective-permute-start | bytes 1572872 | tf_op jit(solution)/shard_map/ppermute | solution.py:29
  0.5 1.9 %collective-permute-start.5 = (bf16[128,512]{1,0:T(8,128)(2,1)}, bf16[128,512]{1,0:T(8,128)(2,1)S(1)}, u32[]{:S(2)}, u32[]{:S(2)}) collective-permute-start(bf16[128,512]{1,0:T(8,128)(2,1)} %refs_1_.2), channel_id=1, source_target_pairs={{0,1},{1,0},{2,3},{3,2},{4,5},{5,4},{6,7},{7,6},{8,9},{9,8},{10,11... | collective-permute-start | bytes 393224 | tf_op jit(solution)/shard_map/ppermute | solution.py:29
  3.8 1.8 %collective-permute-start.6 = (bf16[256,768]{1,0:T(8,128)(2,1)S(1)}, bf16[256,768]{1,0:T(8,128)(2,1)S(1)}, u32[]{:S(2)}, u32[]{:S(2)}) collective-permute-start(bf16[256,768]{1,0:T(8,128)(2,1)S(1)} %get-tuple-element.56.own_ref), channel_id=1, source_target_pairs={{0,1},{1,0},{2,3},{3,2},{4,5},{5,4},{6,7},{7,6},{8,9},{9,8},{10,11... | collective-permute-start | bytes 1179656 | tf_op jit(solution)/shard_map/ppermute | solution.py:29
  8.5 4.5 %copy-start.2 = (s32[1,128]{1,0:T(1,128)S(1)}, s32[1,128]{1,0:T(1,128)}, u32[]{:S(2)}) copy-start(s32[1,128]{1,0:T(1,128)} %refs_1_.3) | copy-start | bytes 1540
  8.5 8.7 %collective-permute-start.17 = (bf16[256,256]{1,0:T(8,128)(2,1)S(1)}, bf16[256,256]{1,0:T(8,128)(2,1)S(1)}, u32[]{:S(2)}, u32[]{:S(2)}) collective-permute-start(bf16[256,256]{1,0:T(8,128)(2,1)S(1)} %get-tuple-element.76), channel_id=1, source_target_pairs={{0,8},{8,0},{16,24},{24,16},{1,9},{9,1},{17,25},{25,17},{2,10},{10... | collective-permute-start | bytes 393224 | tf_op jit(solution)/shard_map/ppermute | solution.py:29
  11.5 2.7 %copy-start.1 = (s32[4,8]{1,0:T(4,128)S(1)}, s32[4,8]{1,0:T(4,128)}, u32[]{:S(2)}) copy-start(s32[4,8]{1,0:T(4,128)} %new_ref.1) | copy-start | bytes 388
  11.5 2.7 %copy-start = (s32[4,4]{1,0:T(4,128)S(1)}, s32[4,4]{1,0:T(4,128)}, u32[]{:S(2)}) copy-start(s32[4,4]{1,0:T(4,128)} %old_ref.1) | copy-start | bytes 196
  11.5 7.4 %collective-permute-start.18 = (bf16[256,256]{1,0:T(8,128)(2,1)S(1)}, bf16[256,256]{1,0:T(8,128)(2,1)S(1)}, u32[]{:S(2)}, u32[]{:S(2)}) collective-permute-start(bf16[256,256]{1,0:T(8,128)(2,1)S(1)} %get-tuple-element.77), channel_id=1, source_target_pairs={{0,16},{8,24},{16,0},{24,8},{1,17},{9,25},{17,1},{25,9},{2,18},{10... | collective-permute-start | bytes 393224 | tf_op jit(solution)/shard_map/ppermute | solution.py:29
  13.0 1.2 %collective-permute-start.1 = (s32[1,128]{1,0:T(1,128)S(1)}, s32[1,128]{1,0:T(1,128)S(1)}, u32[]{:S(2)}, u32[]{:S(2)}) collective-permute-start(s32[1,128]{1,0:T(1,128)S(1)} %copy-done.2), channel_id=1, source_target_pairs={{0,1},{1,0},{2,3},{3,2},{4,5},{5,4},{6,7},{7,6},{8,9},{9,8},{10,11... | collective-permute-start | bytes 1544 | tf_op jit(solution)/shard_map/ppermute | solution.py:29
  13.0 7.6 %collective-permute-start.19 = (bf16[256,256]{1,0:T(8,128)(2,1)S(1)}, bf16[256,256]{1,0:T(8,128)(2,1)S(1)}, u32[]{:S(2)}, u32[]{:S(2)}) collective-permute-start(bf16[256,256]{1,0:T(8,128)(2,1)S(1)} %get-tuple-element.78), channel_id=1, source_target_pairs={{0,24},{8,16},{16,8},{24,0},{1,25},{9,17},{17,9},{25,1},{2,26},{10... | collective-permute-start | bytes 393224 | tf_op jit(solution)/shard_map/ppermute | solution.py:29
  15.1 7.1 %collective-permute-start.2 = (bf16[2,128,256]{2,1,0:T(8,128)(2,1)S(1)}, bf16[2,128,256]{2,1,0:T(8,128)(2,1)S(1)}, u32[]{:S(2)}, u32[]{:S(2)}) collective-permute-start(bf16[2,128,256]{2,1,0:T(8,128)(2,1)S(1)} %get-tuple-element.51), channel_id=1, source_target_pairs={{0,8},{8,0},{16,24},{24,16},{1,9},{9,1},{17,25},{25,17},{2,10},{10... | collective-permute-start | bytes 393224 | tf_op jit(solution)/shard_map/ppermute | solution.py:29
  16.0 9.0 %collective-permute-start.7 = (bf16[256,256]{1,0:T(8,128)(2,1)S(1)}, bf16[256,256]{1,0:T(8,128)(2,1)S(1)}, u32[]{:S(2)}, u32[]{:S(2)}) collective-permute-start(bf16[256,256]{1,0:T(8,128)(2,1)S(1)} %get-tuple-element.60), channel_id=1, source_target_pairs={{0,8},{8,0},{16,24},{24,16},{1,9},{9,1},{17,25},{25,17},{2,10},{10... | collective-permute-start | bytes 393224 | tf_op jit(solution)/shard_map/ppermute | solution.py:29
  17.2 9.3 %collective-permute-start.8 = (bf16[256,256]{1,0:T(8,128)(2,1)S(1)}, bf16[256,256]{1,0:T(8,128)(2,1)S(1)}, u32[]{:S(2)}, u32[]{:S(2)}) collective-permute-start(bf16[256,256]{1,0:T(8,128)(2,1)S(1)} %get-tuple-element.61), channel_id=1, source_target_pairs={{0,16},{8,24},{16,0},{24,8},{1,17},{9,25},{17,1},{25,9},{2,18},{10... | collective-permute-start | bytes 393224 | tf_op jit(solution)/shard_map/ppermute | solution.py:29
  18.9 10.2 %collective-permute-start.9 = (bf16[256,256]{1,0:T(8,128)(2,1)S(1)}, bf16[256,256]{1,0:T(8,128)(2,1)S(1)}, u32[]{:S(2)}, u32[]{:S(2)}) collective-permute-start(bf16[256,256]{1,0:T(8,128)(2,1)S(1)} %get-tuple-element.62), channel_id=1, source_target_pairs={{0,24},{8,16},{16,8},{24,0},{1,25},{9,17},{17,9},{25,1},{2,26},{10... | collective-permute-start | bytes 393224 | tf_op jit(solution)/shard_map/ppermute | solution.py:29
  20.6 11.8 %collective-permute-start.3 = (bf16[2,128,256]{2,1,0:T(8,128)(2,1)S(1)}, bf16[2,128,256]{2,1,0:T(8,128)(2,1)S(1)}, u32[]{:S(2)}, u32[]{:S(2)}) collective-permute-start(bf16[2,128,256]{2,1,0:T(8,128)(2,1)S(1)} %get-tuple-element.52), channel_id=1, source_target_pairs={{0,16},{8,24},{16,0},{24,8},{1,17},{9,25},{17,1},{25,9},{2,18},{10... | collective-permute-start | bytes 393224 | tf_op jit(solution)/shard_map/ppermute | solution.py:29
  22.2 10.8 %collective-permute-start.4 = (bf16[2,128,256]{2,1,0:T(8,128)(2,1)S(1)}, bf16[2,128,256]{2,1,0:T(8,128)(2,1)S(1)}, u32[]{:S(2)}, u32[]{:S(2)}) collective-permute-start(bf16[2,128,256]{2,1,0:T(8,128)(2,1)S(1)} %get-tuple-element.53), channel_id=1, source_target_pairs={{0,24},{8,16},{16,8},{24,0},{1,25},{9,17},{17,9},{25,1},{2,26},{10... | collective-permute-start | bytes 393224 | tf_op jit(solution)/shard_map/ppermute | solution.py:29
  25.0 10.6 %collective-permute-start.20 = (bf16[256,256]{1,0:T(8,128)(2,1)S(1)}, bf16[256,256]{1,0:T(8,128)(2,1)S(1)}, u32[]{:S(2)}, u32[]{:S(2)}) collective-permute-start(bf16[256,256]{1,0:T(8,128)(2,1)S(1)} %get-tuple-element.80), channel_id=1, source_target_pairs={{0,2},{1,3},{2,0},{3,1},{4,6},{5,7},{6,4},{7,5},{8,10},{9,11},{10,... | collective-permute-start | bytes 393224 | tf_op jit(solution)/shard_map/ppermute | solution.py:29
  26.5 11.6 %collective-permute-start.21 = (bf16[256,256]{1,0:T(8,128)(2,1)S(1)}, bf16[256,256]{1,0:T(8,128)(2,1)S(1)}, u32[]{:S(2)}, u32[]{:S(2)}) collective-permute-start(bf16[256,256]{1,0:T(8,128)(2,1)S(1)} %get-tuple-element.81), channel_id=1, source_target_pairs={{0,4},{1,5},{2,6},{3,7},{4,0},{5,1},{6,2},{7,3},{8,12},{9,13},{10,... | collective-permute-start | bytes 393224 | tf_op jit(solution)/shard_map/ppermute | solution.py:29
  29.1 9.9 %collective-permute-start.22 = (bf16[256,256]{1,0:T(8,128)(2,1)S(1)}, bf16[256,256]{1,0:T(8,128)(2,1)S(1)}, u32[]{:S(2)}, u32[]{:S(2)}) collective-permute-start(bf16[256,256]{1,0:T(8,128)(2,1)S(1)} %get-tuple-element.82), channel_id=1, source_target_pairs={{0,6},{1,7},{2,4},{3,5},{4,2},{5,3},{6,0},{7,1},{8,14},{9,15},{10,... | collective-permute-start | bytes 393224 | tf_op jit(solution)/shard_map/ppermute | solution.py:29
  32.5 7.1 %collective-permute-start.10 = (bf16[256,256]{1,0:T(8,128)(2,1)S(1)}, bf16[256,256]{1,0:T(8,128)(2,1)S(1)}, u32[]{:S(2)}, u32[]{:S(2)}) collective-permute-start(bf16[256,256]{1,0:T(8,128)(2,1)S(1)} %get-tuple-element.64), channel_id=1, source_target_pairs={{0,2},{1,3},{2,0},{3,1},{4,6},{5,7},{6,4},{7,5},{8,10},{9,11},{10,... | collective-permute-start | bytes 393224 | tf_op jit(solution)/shard_map/ppermute | solution.py:29
  33.0 16.8 %collective-permute-start.11 = (bf16[256,256]{1,0:T(8,128)(2,1)S(1)}, bf16[256,256]{1,0:T(8,128)(2,1)S(1)}, u32[]{:S(2)}, u32[]{:S(2)}) collective-permute-start(bf16[256,256]{1,0:T(8,128)(2,1)S(1)} %get-tuple-element.65), channel_id=1, source_target_pairs={{0,4},{1,5},{2,6},{3,7},{4,0},{5,1},{6,2},{7,3},{8,12},{9,13},{10,... | collective-permute-start | bytes 393224 | tf_op jit(solution)/shard_map/ppermute | solution.py:29
  35.6 14.2 %collective-permute-start.12 = (bf16[256,256]{1,0:T(8,128)(2,1)S(1)}, bf16[256,256]{1,0:T(8,128)(2,1)S(1)}, u32[]{:S(2)}, u32[]{:S(2)}) collective-permute-start(bf16[256,256]{1,0:T(8,128)(2,1)S(1)} %get-tuple-element.66), channel_id=1, source_target_pairs={{0,6},{1,7},{2,4},{3,5},{4,2},{5,3},{6,0},{7,1},{8,14},{9,15},{10,... | collective-permute-start | bytes 393224 | tf_op jit(solution)/shard_map/ppermute | solution.py:29
  39.3 10.9 %collective-permute-start.23 = (bf16[4,128,256]{2,1,0:T(8,128)(2,1)S(1)}, bf16[4,128,256]{2,1,0:T(8,128)(2,1)S(1)}, u32[]{:S(2)}, u32[]{:S(2)}) collective-permute-start(bf16[4,128,256]{2,1,0:T(8,128)(2,1)S(1)} %get-tuple-element.84), channel_id=1, source_target_pairs={{0,1},{1,0},{2,3},{3,2},{4,5},{5,4},{6,7},{7,6},{8,9},{9,8},{10,11... | collective-permute-start | bytes 786440 | tf_op jit(solution)/shard_map/ppermute | solution.py:29
  50.1 3.7 %collective-permute-start.13 = (bf16[4,128,256]{2,1,0:T(8,128)(2,1)S(1)}, bf16[4,128,256]{2,1,0:T(8,128)(2,1)S(1)}, u32[]{:S(2)}, u32[]{:S(2)}) collective-permute-start(bf16[4,128,256]{2,1,0:T(8,128)(2,1)S(1)} %get-tuple-element.68), channel_id=1, source_target_pairs={{0,1},{1,0},{2,3},{3,2},{4,5},{5,4},{6,7},{7,6},{8,9},{9,8},{10,11... | collective-permute-start | bytes 786440 | tf_op jit(solution)/shard_map/ppermute | solution.py:29
  50.3 6.4 %collective-permute-start.24 = (bf16[128,256]{1,0:T(8,128)(2,1)S(1)}, bf16[128,256]{1,0:T(8,128)(2,1)S(1)}, u32[]{:S(2)}, u32[]{:S(2)}) collective-permute-start(bf16[128,256]{1,0:T(8,128)(2,1)S(1)} %get-tuple-element.86), channel_id=1, source_target_pairs={{0,8},{8,0},{16,24},{24,16},{1,9},{9,1},{17,25},{25,17},{2,10},{10... | collective-permute-start | bytes 196616 | tf_op jit(solution)/shard_map/ppermute | solution.py:29
  51.3 6.2 %collective-permute-start.25 = (bf16[128,256]{1,0:T(8,128)(2,1)S(1)}, bf16[128,256]{1,0:T(8,128)(2,1)S(1)}, u32[]{:S(2)}, u32[]{:S(2)}) collective-permute-start(bf16[128,256]{1,0:T(8,128)(2,1)S(1)} %get-tuple-element.87), channel_id=1, source_target_pairs={{0,16},{8,24},{16,0},{24,8},{1,17},{9,25},{17,1},{25,9},{2,18},{10... | collective-permute-start | bytes 196616 | tf_op jit(solution)/shard_map/ppermute | solution.py:29
  53.1 5.7 %collective-permute-start.26 = (bf16[128,256]{1,0:T(8,128)(2,1)S(1)}, bf16[128,256]{1,0:T(8,128)(2,1)S(1)}, u32[]{:S(2)}, u32[]{:S(2)}) collective-permute-start(bf16[128,256]{1,0:T(8,128)(2,1)S(1)} %get-tuple-element.88), channel_id=1, source_target_pairs={{0,24},{8,16},{16,8},{24,0},{1,25},{9,17},{17,9},{25,1},{2,26},{10... | collective-permute-start | bytes 196616 | tf_op jit(solution)/shard_map/ppermute | solution.py:29
  53.9 4.9 %collective-permute-start.14 = (bf16[128,256]{1,0:T(8,128)(2,1)S(1)}, bf16[128,256]{1,0:T(8,128)(2,1)S(1)}, u32[]{:S(2)}, u32[]{:S(2)}) collective-permute-start(bf16[128,256]{1,0:T(8,128)(2,1)S(1)} %get-tuple-element.70), channel_id=1, source_target_pairs={{0,8},{8,0},{16,24},{24,16},{1,9},{9,1},{17,25},{25,17},{2,10},{10... | collective-permute-start | bytes 196616 | tf_op jit(solution)/shard_map/ppermute | solution.py:29
  54.9 4.6 %collective-permute-start.15 = (bf16[128,256]{1,0:T(8,128)(2,1)S(1)}, bf16[128,256]{1,0:T(8,128)(2,1)S(1)}, u32[]{:S(2)}, u32[]{:S(2)}) collective-permute-start(bf16[128,256]{1,0:T(8,128)(2,1)S(1)} %get-tuple-element.71), channel_id=1, source_target_pairs={{0,16},{8,24},{16,0},{24,8},{1,17},{9,25},{17,1},{25,9},{2,18},{10... | collective-permute-start | bytes 196616 | tf_op jit(solution)/shard_map/ppermute | solution.py:29
  56.7 5.2 %collective-permute-start.16 = (bf16[128,256]{1,0:T(8,128)(2,1)S(1)}, bf16[128,256]{1,0:T(8,128)(2,1)S(1)}, u32[]{:S(2)}, u32[]{:S(2)}) collective-permute-start(bf16[128,256]{1,0:T(8,128)(2,1)S(1)} %get-tuple-element.72), channel_id=1, source_target_pairs={{0,24},{8,16},{16,8},{24,0},{1,25},{9,17},{17,9},{25,1},{2,26},{10... | collective-permute-start | bytes 196616 | tf_op jit(solution)/shard_map/ppermute | solution.py:29
where the time goes:
time: 62.7 us; the launch traced here: 62.6 us
  starting transfers between devices  32.6 us (52%)
  waiting for transfers between devices  20.3 us (32%)
  Pallas kernels  9.55 us (15%)
    ppermute x27, starting transfers between devices, shifted(): return lax.ppermute(shard, axis, [(i, i ^ k * stride) for i in range(size)])  32.6 us
    ppermute x27, waiting for transfers between devices, shifted(): return lax.ppermute(shard, axis, [(i, i ^ k * stride) for i in range(size)])  20.3 us
    pallas_call x13, Pallas kernels, call(): pl.pallas_call(kernel, out_shape=[made[where](*out) for where, out in zip...  9.55 us
  transfers between devices with their start and end apart: 27, of which 13 were waited for; matrix products, arithmetic and copies ran while one was open for 0% of the time, Pallas kernels for 7%

commit v1 on v0

--- a/solution.py
+++ b/solution.py
@@ -134,12 +134,12 @@
     return [slice(start, start + unit * share) for start, share in zip(starts, WIDTHS)]
 
 
-def renew_pieces(model_width, cols, x0_ref, weight_ref, factor, remainder, out_refs):
+def renew_pieces(model_width, cols, which, x0_ref, weight_ref, factor, remainder, out_refs):
     group = own_place()[0]
     chunk = out_refs[0].shape[0]
-    for k in range(len(out_refs)):
+    for k, out_ref in zip(which, out_refs):
         rows = pl.ds(pl.multiple_of((group ^ k) * chunk, chunk), chunk)
-        out_refs[k][...] = renew(
+        out_ref[...] = renew(
             weight_ref[rows, cols],
             x0_ref[rows, :],
             x0_ref[rows, cols],
@@ -152,6 +152,7 @@
 def update_kernel(
     model_width,
     cols,
+    which,
     own_ref,
     peer_ref,
     x0_ref,
@@ -201,12 +202,13 @@
     factor = lax.rsqrt(norm_sq)
     factor_ref[...] = jnp.broadcast_to(factor, factor_ref.shape)
     remainder = remainder_ref[:, cols]
-    renew_pieces(model_width, cols, x0_ref, weight_ref, factor, remainder, out_refs)
-
-
-def later_kernel(model_width, cols, remainder_ref, factor_ref, x0_ref, weight_ref, *out_refs):
+    renew_pieces(model_width, cols, which, x0_ref, weight_ref, factor, remainder, out_refs)
+
+
+def later_kernel(model_width, cols, which, remainder_ref, factor_ref, x0_ref, weight_ref, *out_refs):
     remainder = remainder_ref[:, cols]
-    renew_pieces(model_width, cols, x0_ref, weight_ref, factor_ref[:1, :1], remainder, out_refs)
+    factor = factor_ref[:1, :1]
+    renew_pieces(model_width, cols, which, x0_ref, weight_ref, factor, remainder, out_refs)
 
 
 def choose_kernel(
@@ -242,25 +244,21 @@
         outs[k][...] = store[group ^ plane ^ k]
 
 
-def project_kernel(count, planes, stages, which_ref, *refs):
+def project_kernel(count, planes, stages, rel, which_ref, *refs):
     toks, weights = refs[:count], refs[count : count + planes * stages]
-    keep_ref, send_ref = refs[count + planes * stages :][:2]
-    stores = refs[count + planes * stages + 2 :]
+    out_ref = refs[count + planes * stages]
+    stores = refs[count + planes * stages + 1 :]
     for stage in range(stages):
         for k in range(planes):
             stores[stage][k] = weights[stage * planes + k][...]
-    for rel in (1, 0):
-        for k in range(count):
-            place = which_ref[2 * k + rel]
-            start = 0
-            for store in stores:
-                cols = slice(start, start + store.shape[2])
-                start = cols.stop
-                got = jnp.dot(toks[k][rel], store[place], preferred_element_type=f32)
-                if rel == 0:
-                    keep_ref[k, :, cols] = got
-                else:
-                    send_ref[k, :, cols] = got.astype(bf16)
+    for k in range(count):
+        place = which_ref[2 * k + rel]
+        start = 0
+        for store in stores:
+            cols = slice(start, start + store.shape[2])
+            start = cols.stop
+            got = jnp.dot(toks[k][rel], store[place], preferred_element_type=f32)
+            out_ref[k, :, cols] = got.astype(out_ref.dtype)
 
 
 def join_kernel(count, keep_ref, other_ref, *out_refs):
@@ -379,20 +377,23 @@
     arrived = []
     for stage, cols in enumerate(columns):
         width = cols.stop - cols.start
+        pieces = [None] * count
+        behind = [k for k in range(count) if stage or k != FIRST[0]]
         if stage == 0:
-            remainder, factor, *pieces = call(
-                functools.partial(update_kernel, model_width, cols),
+            remainder, factor, pieces[FIRST[0]] = call(
+                functools.partial(update_kernel, model_width, cols, FIRST[:1]),
                 [own_gram, peer_gram, x0, weight_in],
-                [((hidden, hidden), bf16), ((8, LANES), f32)] + [((chunk, width), bf16)] * count,
+                [((hidden, hidden), bf16), ((8, LANES), f32), ((chunk, width), bf16)],
                 [pltpu.VMEM((hidden, hidden), bf16)] * 4
                 + [pltpu.VMEM((hidden, hidden), f32)] * 3,
             )
-        else:
-            pieces = call(
-                functools.partial(later_kernel, model_width, cols),
-                [remainder, factor, x0, weight_in],
-                [((chunk, width), bf16)] * count,
-            )
+        made = call(
+            functools.partial(later_kernel, model_width, cols, behind),
+            [remainder, factor, x0, weight_in],
+            [((chunk, width), bf16)] * len(behind),
+        )
+        for k, piece in zip(behind, made):
+            pieces[k] = piece
         landed = spread(pieces, "group", 1, FIRST)
         routed = call(
             functools.partial(route_kernel, count),
@@ -407,14 +408,19 @@
     returned = []
     for stages in TAILS:
         widths = [columns[i].stop - columns[i].start for i in stages]
-        keep, send = call(
-            functools.partial(project_kernel, count, planes, len(stages)),
-            [which] + requested + sum((arrived[i] for i in stages), []),
-            [((count, row_count, sum(widths)), f32), ((count, row_count, sum(widths)), bf16)],
-            [pltpu.VMEM((planes, chunk, width), bf16) for width in widths],
-            spaces=[SMEM] + [VMEM] * (count + planes * len(stages)),
-        )
+
+        def projected(rel, dtype):
+            return call(
+                functools.partial(project_kernel, count, planes, len(stages), rel),
+                [which] + requested + sum((arrived[i] for i in stages), []),
+                [((count, row_count, sum(widths)), dtype)],
+                [pltpu.VMEM((planes, chunk, width), bf16) for width in widths],
+                spaces=[SMEM] + [VMEM] * (count + planes * len(stages)),
+            )[0]
+
+        send = projected(1, bf16)
         other = swapped(send)
+        keep = projected(0, f32)
         mine = call(
             functools.partial(join_kernel, count),
             [keep, other],

time: 62.7 us -> 62.3 us (level)
  starting transfers between devices: 32.6 us -> 30.2 us
  waiting for transfers between devices: 20.3 us -> 21.7 us
    ppermute x27, starting transfers between devices: 32.6 us -> 30.2 us  [shifted(): return lax.ppermute(shard, axis, [(i, i ^ k * stride) for i in range(size)])]
    ppermute x27, waiting for transfers between devices: 20.3 us -> 21.7 us  [shifted(): return lax.ppermute(shard, axis, [(i, i ^ k * stride) for i in range(size)])]
    pallas_call x13 -> x16, Pallas kernels: 9.55 us -> 10 us  [call(): pl.pallas_call(kernel, out_shape=[made[where](*out) for where, out in zip...]
  transfers between devices with their start and end apart: 27 -> 27, of which waited for: 13 -> 11; matrix products, arithmetic and copies ran while one was open for 0% -> 0% of each run, Pallas kernels for 7% -> 9%
where the time goes in v1:
time: 62.3 us; the launch traced here: 62.2 us
  starting transfers between devices  30.2 us (48%)
  waiting for transfers between devices  21.7 us (35%)
  Pallas kernels  10 us (16%)
    ppermute x27, starting transfers between devices, shifted(): return lax.ppermute(shard, axis, [(i, i ^ k * stride) for i in range(size)])  30.2 us
    ppermute x27, waiting for transfers between devices, shifted(): return lax.ppermute(shard, axis, [(i, i ^ k * stride) for i in range(size)])  21.7 us
    pallas_call x16, Pallas kernels, call(): pl.pallas_call(kernel, out_shape=[made[where](*out) for where, out in zip...  10 us
  transfers between devices with their start and end apart: 27, of which 11 were waited for; matrix products, arithmetic and copies ran while one was open for 0% of the time, Pallas kernels for 9%

profile of v1, /device:TPU:0, one launch (start us, length us, event | category | flops | bytes accessed | tf_op | source)
XLA Modules:
  0.0 62.2 jit_solution(9891625581334999081)
XLA Ops:
  0.0 0.5 collective-permute-start
  0.5 0.0 collective-permute-start.5
  0.5 1.5 %shard_map.73 = (bf16[128,2048]{1,0:T(8,128)(2,1)S(1)}, bf16[128,512]{1,0:T(8,128)(2,1)S(1)}, bf16[1024,512]{1,0:T(8,128)(2,1)S(1)}) custom-call(bf16[128,2048]{1,0:T(8,128)(2,1)} %refs_0_.1, bf16[128,512]{1,0:T(8,128)(2,1)} %refs_1_.2, bf16[1024,512]{1,0:T(8,128)(2,1)} %bitcast.3), custom_call_target="tpu_custom_call" | custom-call | tf_op jit(solution)/shard_map/pallas_call | solution.py:290
  2.0 0.5 collective-permute-done.5.peer_cot_ref
  2.4 0.0 collective-permute-done.peer_ref
  2.4 1.4 %shard_map.76 = (bf16[1024,512]{1,0:T(8,128)(2,1)S(1)}, bf16[256,768]{1,0:T(8,128)(2,1)S(1)}) custom-call(bf16[128,2048]{1,0:T(8,128)(2,1)S(1)} %get-tuple-element.43.own_ref, bf16[128,2048]{1,0:T(8,128)(2,1)S(1)} %collective-permute-done.peer_ref, bf16[128,512]{1,0:T(8,128)(2,1)S(1)} %get-tuple-element.50.cot_ref, ...), custom_call_target="tpu_custom_call" | custom-call | tf_op jit(solution)/shard_map/pallas_call | solution.py:290
  3.8 0.4 collective-permute-start.6
  4.2 1.2 %shard_map.74 = (bf16[1024,512]{1,0:T(8,128)(2,1)S(1)}, s32[1,128]{1,0:T(1,128)S(1)}) custom-call(bf16[1024,512]{1,0:T(8,128)(2,1)} %bitcast.2, s32[1,128]{1,0:T(1,128)} %refs_1_.3), custom_call_target="tpu_custom_call" | custom-call | tf_op jit(solution)/shard_map/pallas_call | solution.py:290
  5.5 0.1 collective-permute-done.6.peer_ref
  5.6 2.1 %shard_map.77 = (bf16[512,512]{1,0:T(8,128)(2,1)S(1)}, f32[8,128]{1,0:T(8,128)S(1)}, bf16[256,256]{1,0:T(8,128)(2,1)S(1)}) custom-call(bf16[256,768]{1,0:T(8,128)(2,1)S(1)} %get-tuple-element.52.own_ref, bf16[256,768]{1,0:T(8,128)(2,1)S(1)} %collective-permute-done.6.peer_ref, bf16[1024,512]{1,0:T(8,128)(2,1)S(1)} %get-tuple-element.53.x0_ref, ...), custom_call_target="tpu_custom_call" | custom-call | tf_op jit(solution)/shard_map/pallas_call | solution.py:290
  7.7 3.9 %collective-permute-start.9 = (bf16[256,256]{1,0:T(8,128)(2,1)S(1)}, bf16[256,256]{1,0:T(8,128)(2,1)S(1)}, u32[]{:S(2)}, u32[]{:S(2)}) collective-permute-start(bf16[256,256]{1,0:T(8,128)(2,1)S(1)} %get-tuple-element.60), channel_id=1, source_target_pairs={{0,24},{8,16},{16,8},{24,0},{1,25},{9,17},{17,9},{25,1},{2,26},{10... | collective-permute-start | bytes 393224 | tf_op jit(solution)/shard_map/ppermute | solution.py:29
  11.6 0.4 shard_map.78
  12.0 0.0 copy-start.1
  12.0 0.0 copy-start
  12.0 0.6 collective-permute-start.7
  12.6 0.1 collective-permute-start.8
  12.8 1.0 %collective-permute-done.1.peer_ids_ref = s32[1,128]{1,0:T(1,128)S(1)} collective-permute-done((s32[1,128]{1,0:T(1,128)S(1)}, s32[1,128]{1,0:T(1,128)S(1)}, u32[]{:S(2)}, u32[]{:S(2)}) %collective-permute-start.1) | collective-permute-done | bytes 544 | tf_op jit(solution)/shard_map/ppermute | solution.py:29
  13.8 0.9 %shard_map.75 = (s32[8]{0:T(128)S(4)}, bf16[2,128,256]{2,1,0:T(8,128)(2,1)S(1)}, bf16[2,128,256]{2,1,0:T(8,128)(2,1)S(1)}, bf16[2,128,256]{2,1,0:T(8,128)(2,1)S(1)}, bf16[2,128,256]{2,1,0:T(8,128)(2,1)S(1)}) custom-call(s32[4,4]{1,0:T(4,128)S(1)} %copy-done, s32[4,8]{1,0:T(4,128)S(1)} %copy-done.1, bf16[128,2048]{1,0:T(8,128)(2,1)S(1)} %get-tuple-element.43.own_ref, ...), custom_call_target="tpu_custom_call" | custom-call | tf_op jit(solution)/shard_map/pallas_call | solution.py:290
  14.7 1.6 %collective-permute-start.2 = (bf16[2,128,256]{2,1,0:T(8,128)(2,1)S(1)}, bf16[2,128,256]{2,1,0:T(8,128)(2,1)S(1)}, u32[]{:S(2)}, u32[]{:S(2)}) collective-permute-start(bf16[2,128,256]{2,1,0:T(8,128)(2,1)S(1)} %get-tuple-element.47), channel_id=1, source_target_pairs={{0,8},{8,0},{16,24},{24,16},{1,9},{9,1},{17,25},{25,17},{2,10},{10... | collective-permute-start | bytes 393224 | tf_op jit(solution)/shard_map/ppermute | solution.py:29
  16.3 0.5 shard_map.83
  16.8 0.6 collective-permute-start.17
  17.4 0.9 %collective-permute-start.18 = (bf16[256,256]{1,0:T(8,128)(2,1)S(1)}, bf16[256,256]{1,0:T(8,128)(2,1)S(1)}, u32[]{:S(2)}, u32[]{:S(2)}) collective-permute-start(bf16[256,256]{1,0:T(8,128)(2,1)S(1)} %get-tuple-element.71), channel_id=1, source_target_pairs={{0,16},{8,24},{16,0},{24,8},{1,17},{9,25},{17,1},{25,9},{2,18},{10... | collective-permute-start | bytes 393224 | tf_op jit(solution)/shard_map/ppermute | solution.py:29
  18.3 1.0 %collective-permute-done.7.refs_1_ = bf16[256,256]{1,0:T(8,128)(2,1)S(1)} collective-permute-done((bf16[256,256]{1,0:T(8,128)(2,1)S(1)}, bf16[256,256]{1,0:T(8,128)(2,1)S(1)}, u32[]{:S(2)}, u32[]{:S(2)}) %collective-permute-start.7) | collective-permute-done | bytes 131104 | tf_op jit(solution)/shard_map/ppermute | solution.py:29
  19.3 1.1 %collective-permute-start.19 = (bf16[256,256]{1,0:T(8,128)(2,1)S(1)}, bf16[256,256]{1,0:T(8,128)(2,1)S(1)}, u32[]{:S(2)}, u32[]{:S(2)}) collective-permute-start(bf16[256,256]{1,0:T(8,128)(2,1)S(1)} %get-tuple-element.72), channel_id=1, source_target_pairs={{0,24},{8,16},{16,8},{24,0},{1,25},{9,17},{17,9},{25,1},{2,26},{10... | collective-permute-start | bytes 393224 | tf_op jit(solution)/shard_map/ppermute | solution.py:29
  20.4 0.0 collective-permute-done.8.refs_2_
  20.4 1.9 %collective-permute-start.3 = (bf16[2,128,256]{2,1,0:T(8,128)(2,1)S(1)}, bf16[2,128,256]{2,1,0:T(8,128)(2,1)S(1)}, u32[]{:S(2)}, u32[]{:S(2)}) collective-permute-start(bf16[2,128,256]{2,1,0:T(8,128)(2,1)S(1)} %get-tuple-element.48), channel_id=1, source_target_pairs={{0,16},{8,24},{16,0},{24,8},{1,17},{9,25},{17,1},{25,9},{2,18},{10... | collective-permute-start | bytes 393224 | tf_op jit(solution)/shard_map/ppermute | solution.py:29
  22.3 0.1 shard_map.79
  22.3 0.8 %collective-permute-start.4 = (bf16[2,128,256]{2,1,0:T(8,128)(2,1)S(1)}, bf16[2,128,256]{2,1,0:T(8,128)(2,1)S(1)}, u32[]{:S(2)}, u32[]{:S(2)}) collective-permute-start(bf16[2,128,256]{2,1,0:T(8,128)(2,1)S(1)} %get-tuple-element.49), channel_id=1, source_target_pairs={{0,24},{8,16},{16,8},{24,0},{1,25},{9,17},{17,9},{25,1},{2,26},{10... | collective-permute-start | bytes 393224 | tf_op jit(solution)/shard_map/ppermute | solution.py:29
  23.1 1.8 %collective-permute-done.17.refs_1_ = bf16[256,256]{1,0:T(8,128)(2,1)S(1)} collective-permute-done((bf16[256,256]{1,0:T(8,128)(2,1)S(1)}, bf16[256,256]{1,0:T(8,128)(2,1)S(1)}, u32[]{:S(2)}, u32[]{:S(2)}) %collective-permute-start.17) | collective-permute-done | bytes 131104 | tf_op jit(solution)/shard_map/ppermute | solution.py:29
  24.9 1.6 %collective-permute-start.10 = (bf16[256,256]{1,0:T(8,128)(2,1)S(1)}, bf16[256,256]{1,0:T(8,128)(2,1)S(1)}, u32[]{:S(2)}, u32[]{:S(2)}) collective-permute-start(bf16[256,256]{1,0:T(8,128)(2,1)S(1)} %get-tuple-element.62), channel_id=1, source_target_pairs={{0,2},{1,3},{2,0},{3,1},{4,6},{5,7},{6,4},{7,5},{8,10},{9,11},{10,... | collective-permute-start | bytes 393224 | tf_op jit(solution)/shard_map/ppermute | solution.py:29
  26.5 0.0 collective-permute-done.18.refs_2_
  26.5 2.6 %collective-permute-start.11 = (bf16[256,256]{1,0:T(8,128)(2,1)S(1)}, bf16[256,256]{1,0:T(8,128)(2,1)S(1)}, u32[]{:S(2)}, u32[]{:S(2)}) collective-permute-start(bf16[256,256]{1,0:T(8,128)(2,1)S(1)} %get-tuple-element.63), channel_id=1, source_target_pairs={{0,4},{1,5},{2,6},{3,7},{4,0},{5,1},{6,2},{7,3},{8,12},{9,13},{10,... | collective-permute-start | bytes 393224 | tf_op jit(solution)/shard_map/ppermute | solution.py:29
  29.1 2.0 %collective-permute-start.12 = (bf16[256,256]{1,0:T(8,128)(2,1)S(1)}, bf16[256,256]{1,0:T(8,128)(2,1)S(1)}, u32[]{:S(2)}, u32[]{:S(2)}) collective-permute-start(bf16[256,256]{1,0:T(8,128)(2,1)S(1)} %get-tuple-element.64), channel_id=1, source_target_pairs={{0,6},{1,7},{2,4},{3,5},{4,2},{5,3},{6,0},{7,1},{8,14},{9,15},{10,... | collective-permute-start | bytes 393224 | tf_op jit(solution)/shard_map/ppermute | solution.py:29
  31.0 0.1 shard_map.84
  31.1 0.0 collective-permute-done.3.refs_2_
  31.1 1.3 %collective-permute-start.20 = (bf16[256,256]{1,0:T(8,128)(2,1)S(1)}, bf16[256,256]{1,0:T(8,128)(2,1)S(1)}, u32[]{:S(2)}, u32[]{:S(2)}) collective-permute-start(bf16[256,256]{1,0:T(8,128)(2,1)S(1)} %get-tuple-element.74), channel_id=1, source_target_pairs={{0,2},{1,3},{2,0},{3,1},{4,6},{5,7},{6,4},{7,5},{8,10},{9,11},{10,... | collective-permute-start | bytes 393224 | tf_op jit(solution)/shard_map/ppermute | solution.py:29
  32.4 0.0 collective-permute-done.4.refs_3_
  32.4 2.6 %collective-permute-start.21 = (bf16[256,256]{1,0:T(8,128)(2,1)S(1)}, bf16[256,256]{1,0:T(8,128)(2,1)S(1)}, u32[]{:S(2)}, u32[]{:S(2)}) collective-permute-start(bf16[256,256]{1,0:T(8,128)(2,1)S(1)} %get-tuple-element.75), channel_id=1, source_target_pairs={{0,4},{1,5},{2,6},{3,7},{4,0},{5,1},{6,2},{7,3},{8,12},{9,13},{10,... | collective-permute-start | bytes 393224 | tf_op jit(solution)/shard_map/ppermute | solution.py:29
  35.0 0.0 collective-permute-done.10.refs_5_
  35.0 0.6 collective-permute-start.22
  35.6 3.5 %collective-permute-done.11.refs_6_ = bf16[256,256]{1,0:T(8,128)(2,1)S(1)} collective-permute-done((bf16[256,256]{1,0:T(8,128)(2,1)S(1)}, bf16[256,256]{1,0:T(8,128)(2,1)S(1)}, u32[]{:S(2)}, u32[]{:S(2)}) %collective-permute-start.11) | collective-permute-done | bytes 131104 | tf_op jit(solution)/shard_map/ppermute | solution.py:29
  39.1 0.0 collective-permute-done.12.refs_7_
  39.1 0.3 shard_map.81
  39.4 0.1 collective-permute-start.13
  39.5 0.0 collective-permute-done.20.refs_5_
  39.5 9.7 %collective-permute-done.21.refs_6_ = bf16[256,256]{1,0:T(8,128)(2,1)S(1)} collective-permute-done((bf16[256,256]{1,0:T(8,128)(2,1)S(1)}, bf16[256,256]{1,0:T(8,128)(2,1)S(1)}, u32[]{:S(2)}, u32[]{:S(2)}) %collective-permute-start.21) | collective-permute-done | bytes 131104 | tf_op jit(solution)/shard_map/ppermute | solution.py:29
  49.2 0.0 collective-permute-done.22.refs_7_
  49.2 0.3 shard_map.86
  49.5 0.1 collective-permute-start.23
  49.6 0.3 shard_map.80.keep_ref
  49.9 0.0 collective-permute-done.13.other_ref
  49.9 1.6 %collective-permute-start.14 = (bf16[128,256]{1,0:T(8,128)(2,1)S(1)}, bf16[128,256]{1,0:T(8,128)(2,1)S(1)}, u32[]{:S(2)}, u32[]{:S(2)}) collective-permute-start(bf16[128,256]{1,0:T(8,128)(2,1)S(1)} %get-tuple-element.66), channel_id=1, source_target_pairs={{0,8},{8,0},{16,24},{24,16},{1,9},{9,1},{17,25},{25,17},{2,10},{10... | collective-permute-start | bytes 196616 | tf_op jit(solution)/shard_map/ppermute | solution.py:29
  51.5 0.3 shard_map.85.keep_ref
  51.7 0.9 %collective-permute-start.15 = (bf16[128,256]{1,0:T(8,128)(2,1)S(1)}, bf16[128,256]{1,0:T(8,128)(2,1)S(1)}, u32[]{:S(2)}, u32[]{:S(2)}) collective-permute-start(bf16[128,256]{1,0:T(8,128)(2,1)S(1)} %get-tuple-element.67), channel_id=1, source_target_pairs={{0,16},{8,24},{16,0},{24,8},{1,17},{9,25},{17,1},{25,9},{2,18},{10... | collective-permute-start | bytes 196616 | tf_op jit(solution)/shard_map/ppermute | solution.py:29
  52.7 1.1 %collective-permute-start.16 = (bf16[128,256]{1,0:T(8,128)(2,1)S(1)}, bf16[128,256]{1,0:T(8,128)(2,1)S(1)}, u32[]{:S(2)}, u32[]{:S(2)}) collective-permute-start(bf16[128,256]{1,0:T(8,128)(2,1)S(1)} %get-tuple-element.68), channel_id=1, source_target_pairs={{0,24},{8,16},{16,8},{24,0},{1,25},{9,17},{17,9},{25,1},{2,26},{10... | collective-permute-start | bytes 196616 | tf_op jit(solution)/shard_map/ppermute | solution.py:29
  53.8 0.0 collective-permute-done.23.other_ref
  53.9 1.6 %collective-permute-start.24 = (bf16[128,256]{1,0:T(8,128)(2,1)S(1)}, bf16[128,256]{1,0:T(8,128)(2,1)S(1)}, u32[]{:S(2)}, u32[]{:S(2)}) collective-permute-start(bf16[128,256]{1,0:T(8,128)(2,1)S(1)} %get-tuple-element.78), channel_id=1, source_target_pairs={{0,8},{8,0},{16,24},{24,16},{1,9},{9,1},{17,25},{25,17},{2,10},{10... | collective-permute-start | bytes 196616 | tf_op jit(solution)/shard_map/ppermute | solution.py:29
  55.4 0.9 %collective-permute-start.25 = (bf16[128,256]{1,0:T(8,128)(2,1)S(1)}, bf16[128,256]{1,0:T(8,128)(2,1)S(1)}, u32[]{:S(2)}, u32[]{:S(2)}) collective-permute-start(bf16[128,256]{1,0:T(8,128)(2,1)S(1)} %get-tuple-element.79), channel_id=1, source_target_pairs={{0,16},{8,24},{16,0},{24,8},{1,17},{9,25},{17,1},{25,9},{2,18},{10... | collective-permute-start | bytes 196616 | tf_op jit(solution)/shard_map/ppermute | solution.py:29
  56.3 1.1 %collective-permute-start.26 = (bf16[128,256]{1,0:T(8,128)(2,1)S(1)}, bf16[128,256]{1,0:T(8,128)(2,1)S(1)}, u32[]{:S(2)}, u32[]{:S(2)}) collective-permute-start(bf16[128,256]{1,0:T(8,128)(2,1)S(1)} %get-tuple-element.80), channel_id=1, source_target_pairs={{0,24},{8,16},{16,8},{24,0},{1,25},{9,17},{17,9},{25,1},{2,26},{10... | collective-permute-start | bytes 196616 | tf_op jit(solution)/shard_map/ppermute | solution.py:29
  57.4 0.9 %collective-permute-done.16.refs_3_ = bf16[128,256]{1,0:T(8,128)(2,1)S(1)} collective-permute-done((bf16[128,256]{1,0:T(8,128)(2,1)S(1)}, bf16[128,256]{1,0:T(8,128)(2,1)S(1)}, u32[]{:S(2)}, u32[]{:S(2)}) %collective-permute-start.16) | collective-permute-done | bytes 65568 | tf_op jit(solution)/shard_map/ppermute | solution.py:29
  58.3 0.3 collective-permute-done.24.refs_5_
  58.6 1.7 %collective-permute-done.25.refs_6_ = bf16[128,256]{1,0:T(8,128)(2,1)S(1)} collective-permute-done((bf16[128,256]{1,0:T(8,128)(2,1)S(1)}, bf16[128,256]{1,0:T(8,128)(2,1)S(1)}, u32[]{:S(2)}, u32[]{:S(2)}) %collective-permute-start.25) | collective-permute-done | bytes 65568 | tf_op jit(solution)/shard_map/ppermute | solution.py:29
  60.3 1.1 %collective-permute-done.26.refs_7_ = bf16[128,256]{1,0:T(8,128)(2,1)S(1)} collective-permute-done((bf16[128,256]{1,0:T(8,128)(2,1)S(1)}, bf16[128,256]{1,0:T(8,128)(2,1)S(1)}, u32[]{:S(2)}, u32[]{:S(2)}) %collective-permute-start.26) | collective-permute-done | bytes 65568 | tf_op jit(solution)/shard_map/ppermute | solution.py:29
  61.4 0.7 %shard_map.88 = bf16[128,512]{1,0:T(8,128)(2,1)} custom-call(bf16[128,256]{1,0:T(8,128)(2,1)S(1)} %get-tuple-element.65.refs_0_, bf16[128,256]{1,0:T(8,128)(2,1)S(1)} %collective-permute-done.14.refs_1_, bf16[128,256]{1,0:T(8,128)(2,1)S(1)} %collective-permute-done.15.refs_2_, bf16[128,256]{1,0:T(8,128)(2,1)S(1)} %collective-permute-done.16.refs_3_, ...), custom_call_target="tpu_custom_call" | custom-call | tf_op jit(solution)/shard_map/pallas_call | solution.py:290
  (12 shorter events, 0.1 us)
Async XLA Ops:
  0.0 2.4 %collective-permute-start = (bf16[128,2048]{1,0:T(8,128)(2,1)}, bf16[128,2048]{1,0:T(8,128)(2,1)S(1)}, u32[]{:S(2)}, u32[]{:S(2)}) collective-permute-start(bf16[128,2048]{1,0:T(8,128)(2,1)} %refs_0_.1), channel_id=1, source_target_pairs={{0,1},{1,0},{2,3},{3,2},{4,5},{5,4},{6,7},{7,6},{8,9},{9,8},{10,11... | collective-permute-start | bytes 1572872 | tf_op jit(solution)/shard_map/ppermute | solution.py:29
  0.5 1.9 %collective-permute-start.5 = (bf16[128,512]{1,0:T(8,128)(2,1)}, bf16[128,512]{1,0:T(8,128)(2,1)S(1)}, u32[]{:S(2)}, u32[]{:S(2)}) collective-permute-start(bf16[128,512]{1,0:T(8,128)(2,1)} %refs_1_.2), channel_id=1, source_target_pairs={{0,1},{1,0},{2,3},{3,2},{4,5},{5,4},{6,7},{7,6},{8,9},{9,8},{10,11... | collective-permute-start | bytes 393224 | tf_op jit(solution)/shard_map/ppermute | solution.py:29
  3.8 1.8 %collective-permute-start.6 = (bf16[256,768]{1,0:T(8,128)(2,1)S(1)}, bf16[256,768]{1,0:T(8,128)(2,1)S(1)}, u32[]{:S(2)}, u32[]{:S(2)}) collective-permute-start(bf16[256,768]{1,0:T(8,128)(2,1)S(1)} %get-tuple-element.52.own_ref), channel_id=1, source_target_pairs={{0,1},{1,0},{2,3},{3,2},{4,5},{5,4},{6,7},{7,6},{8,9},{9,8},{10,11... | collective-permute-start | bytes 1179656 | tf_op jit(solution)/shard_map/ppermute | solution.py:29
  7.7 9.7 %collective-permute-start.9 = (bf16[256,256]{1,0:T(8,128)(2,1)S(1)}, bf16[256,256]{1,0:T(8,128)(2,1)S(1)}, u32[]{:S(2)}, u32[]{:S(2)}) collective-permute-start(bf16[256,256]{1,0:T(8,128)(2,1)S(1)} %get-tuple-element.60), channel_id=1, source_target_pairs={{0,24},{8,16},{16,8},{24,0},{1,25},{9,17},{17,9},{25,1},{2,26},{10... | collective-permute-start | bytes 393224 | tf_op jit(solution)/shard_map/ppermute | solution.py:29
  11.6 1.0 %copy-start.2 = (s32[1,128]{1,0:T(1,128)S(1)}, s32[1,128]{1,0:T(1,128)}, u32[]{:S(2)}) copy-start(s32[1,128]{1,0:T(1,128)} %refs_1_.3) | copy-start | bytes 1540
  12.0 1.8 %copy-start.1 = (s32[4,8]{1,0:T(4,128)S(1)}, s32[4,8]{1,0:T(4,128)}, u32[]{:S(2)}) copy-start(s32[4,8]{1,0:T(4,128)} %new_ref.1) | copy-start | bytes 388
  12.0 1.8 %copy-start = (s32[4,4]{1,0:T(4,128)S(1)}, s32[4,4]{1,0:T(4,128)}, u32[]{:S(2)}) copy-start(s32[4,4]{1,0:T(4,128)} %old_ref.1) | copy-start | bytes 196
  12.0 7.2 %collective-permute-start.7 = (bf16[256,256]{1,0:T(8,128)(2,1)S(1)}, bf16[256,256]{1,0:T(8,128)(2,1)S(1)}, u32[]{:S(2)}, u32[]{:S(2)}) collective-permute-start(bf16[256,256]{1,0:T(8,128)(2,1)S(1)} %get-tuple-element.58), channel_id=1, source_target_pairs={{0,8},{8,0},{16,24},{24,16},{1,9},{9,1},{17,25},{25,17},{2,10},{10... | collective-permute-start | bytes 393224 | tf_op jit(solution)/shard_map/ppermute | solution.py:29
  12.6 1.2 %collective-permute-start.1 = (s32[1,128]{1,0:T(1,128)S(1)}, s32[1,128]{1,0:T(1,128)S(1)}, u32[]{:S(2)}, u32[]{:S(2)}) collective-permute-start(s32[1,128]{1,0:T(1,128)S(1)} %copy-done.2), channel_id=1, source_target_pairs={{0,1},{1,0},{2,3},{3,2},{4,5},{5,4},{6,7},{7,6},{8,9},{9,8},{10,11... | collective-permute-start | bytes 1544 | tf_op jit(solution)/shard_map/ppermute | solution.py:29
  12.6 7.8 %collective-permute-start.8 = (bf16[256,256]{1,0:T(8,128)(2,1)S(1)}, bf16[256,256]{1,0:T(8,128)(2,1)S(1)}, u32[]{:S(2)}, u32[]{:S(2)}) collective-permute-start(bf16[256,256]{1,0:T(8,128)(2,1)S(1)} %get-tuple-element.59), channel_id=1, source_target_pairs={{0,16},{8,24},{16,0},{24,8},{1,17},{9,25},{17,1},{25,9},{2,18},{10... | collective-permute-start | bytes 393224 | tf_op jit(solution)/shard_map/ppermute | solution.py:29
  14.7 7.6 %collective-permute-start.2 = (bf16[2,128,256]{2,1,0:T(8,128)(2,1)S(1)}, bf16[2,128,256]{2,1,0:T(8,128)(2,1)S(1)}, u32[]{:S(2)}, u32[]{:S(2)}) collective-permute-start(bf16[2,128,256]{2,1,0:T(8,128)(2,1)S(1)} %get-tuple-element.47), channel_id=1, source_target_pairs={{0,8},{8,0},{16,24},{24,16},{1,9},{9,1},{17,25},{25,17},{2,10},{10... | collective-permute-start | bytes 393224 | tf_op jit(solution)/shard_map/ppermute | solution.py:29
  16.8 8.1 %collective-permute-start.17 = (bf16[256,256]{1,0:T(8,128)(2,1)S(1)}, bf16[256,256]{1,0:T(8,128)(2,1)S(1)}, u32[]{:S(2)}, u32[]{:S(2)}) collective-permute-start(bf16[256,256]{1,0:T(8,128)(2,1)S(1)} %get-tuple-element.70), channel_id=1, source_target_pairs={{0,8},{8,0},{16,24},{24,16},{1,9},{9,1},{17,25},{25,17},{2,10},{10... | collective-permute-start | bytes 393224 | tf_op jit(solution)/shard_map/ppermute | solution.py:29
  17.4 9.1 %collective-permute-start.18 = (bf16[256,256]{1,0:T(8,128)(2,1)S(1)}, bf16[256,256]{1,0:T(8,128)(2,1)S(1)}, u32[]{:S(2)}, u32[]{:S(2)}) collective-permute-start(bf16[256,256]{1,0:T(8,128)(2,1)S(1)} %get-tuple-element.71), channel_id=1, source_target_pairs={{0,16},{8,24},{16,0},{24,8},{1,17},{9,25},{17,1},{25,9},{2,18},{10... | collective-permute-start | bytes 393224 | tf_op jit(solution)/shard_map/ppermute | solution.py:29
  19.3 9.8 %collective-permute-start.19 = (bf16[256,256]{1,0:T(8,128)(2,1)S(1)}, bf16[256,256]{1,0:T(8,128)(2,1)S(1)}, u32[]{:S(2)}, u32[]{:S(2)}) collective-permute-start(bf16[256,256]{1,0:T(8,128)(2,1)S(1)} %get-tuple-element.72), channel_id=1, source_target_pairs={{0,24},{8,16},{16,8},{24,0},{1,25},{9,17},{17,9},{25,1},{2,26},{10... | collective-permute-start | bytes 393224 | tf_op jit(solution)/shard_map/ppermute | solution.py:29
  20.4 10.7 %collective-permute-start.3 = (bf16[2,128,256]{2,1,0:T(8,128)(2,1)S(1)}, bf16[2,128,256]{2,1,0:T(8,128)(2,1)S(1)}, u32[]{:S(2)}, u32[]{:S(2)}) collective-permute-start(bf16[2,128,256]{2,1,0:T(8,128)(2,1)S(1)} %get-tuple-element.48), channel_id=1, source_target_pairs={{0,16},{8,24},{16,0},{24,8},{1,17},{9,25},{17,1},{25,9},{2,18},{10... | collective-permute-start | bytes 393224 | tf_op jit(solution)/shard_map/ppermute | solution.py:29
  22.3 10.1 %collective-permute-start.4 = (bf16[2,128,256]{2,1,0:T(8,128)(2,1)S(1)}, bf16[2,128,256]{2,1,0:T(8,128)(2,1)S(1)}, u32[]{:S(2)}, u32[]{:S(2)}) collective-permute-start(bf16[2,128,256]{2,1,0:T(8,128)(2,1)S(1)} %get-tuple-element.49), channel_id=1, source_target_pairs={{0,24},{8,16},{16,8},{24,0},{1,25},{9,17},{17,9},{25,1},{2,26},{10... | collective-permute-start | bytes 393224 | tf_op jit(solution)/shard_map/ppermute | solution.py:29
  24.9 10.1 %collective-permute-start.10 = (bf16[256,256]{1,0:T(8,128)(2,1)S(1)}, bf16[256,256]{1,0:T(8,128)(2,1)S(1)}, u32[]{:S(2)}, u32[]{:S(2)}) collective-permute-start(bf16[256,256]{1,0:T(8,128)(2,1)S(1)} %get-tuple-element.62), channel_id=1, source_target_pairs={{0,2},{1,3},{2,0},{3,1},{4,6},{5,7},{6,4},{7,5},{8,10},{9,11},{10,... | collective-permute-start | bytes 393224 | tf_op jit(solution)/shard_map/ppermute | solution.py:29
  26.5 12.6 %collective-permute-start.11 = (bf16[256,256]{1,0:T(8,128)(2,1)S(1)}, bf16[256,256]{1,0:T(8,128)(2,1)S(1)}, u32[]{:S(2)}, u32[]{:S(2)}) collective-permute-start(bf16[256,256]{1,0:T(8,128)(2,1)S(1)} %get-tuple-element.63), channel_id=1, source_target_pairs={{0,4},{1,5},{2,6},{3,7},{4,0},{5,1},{6,2},{7,3},{8,12},{9,13},{10,... | collective-permute-start | bytes 393224 | tf_op jit(solution)/shard_map/ppermute | solution.py:29
  29.1 10.1 %collective-permute-start.12 = (bf16[256,256]{1,0:T(8,128)(2,1)S(1)}, bf16[256,256]{1,0:T(8,128)(2,1)S(1)}, u32[]{:S(2)}, u32[]{:S(2)}) collective-permute-start(bf16[256,256]{1,0:T(8,128)(2,1)S(1)} %get-tuple-element.64), channel_id=1, source_target_pairs={{0,6},{1,7},{2,4},{3,5},{4,2},{5,3},{6,0},{7,1},{8,14},{9,15},{10,... | collective-permute-start | bytes 393224 | tf_op jit(solution)/shard_map/ppermute | solution.py:29
  31.1 8.4 %collective-permute-start.20 = (bf16[256,256]{1,0:T(8,128)(2,1)S(1)}, bf16[256,256]{1,0:T(8,128)(2,1)S(1)}, u32[]{:S(2)}, u32[]{:S(2)}) collective-permute-start(bf16[256,256]{1,0:T(8,128)(2,1)S(1)} %get-tuple-element.74), channel_id=1, source_target_pairs={{0,2},{1,3},{2,0},{3,1},{4,6},{5,7},{6,4},{7,5},{8,10},{9,11},{10,... | collective-permute-start | bytes 393224 | tf_op jit(solution)/shard_map/ppermute | solution.py:29
  32.4 16.8 %collective-permute-start.21 = (bf16[256,256]{1,0:T(8,128)(2,1)S(1)}, bf16[256,256]{1,0:T(8,128)(2,1)S(1)}, u32[]{:S(2)}, u32[]{:S(2)}) collective-permute-start(bf16[256,256]{1,0:T(8,128)(2,1)S(1)} %get-tuple-element.75), channel_id=1, source_target_pairs={{0,4},{1,5},{2,6},{3,7},{4,0},{5,1},{6,2},{7,3},{8,12},{9,13},{10,... | collective-permute-start | bytes 393224 | tf_op jit(solution)/shard_map/ppermute | solution.py:29
  35.0 14.2 %collective-permute-start.22 = (bf16[256,256]{1,0:T(8,128)(2,1)S(1)}, bf16[256,256]{1,0:T(8,128)(2,1)S(1)}, u32[]{:S(2)}, u32[]{:S(2)}) collective-permute-start(bf16[256,256]{1,0:T(8,128)(2,1)S(1)} %get-tuple-element.76), channel_id=1, source_target_pairs={{0,6},{1,7},{2,4},{3,5},{4,2},{5,3},{6,0},{7,1},{8,14},{9,15},{10,... | collective-permute-start | bytes 393224 | tf_op jit(solution)/shard_map/ppermute | solution.py:29
  39.4 10.4 %collective-permute-start.13 = (bf16[4,128,256]{2,1,0:T(8,128)(2,1)S(1)}, bf16[4,128,256]{2,1,0:T(8,128)(2,1)S(1)}, u32[]{:S(2)}, u32[]{:S(2)}) collective-permute-start(bf16[4,128,256]{2,1,0:T(8,128)(2,1)S(1)} %shard_map.81), channel_id=1, source_target_pairs={{0,1},{1,0},{2,3},{3,2},{4,5},{5,4},{6,7},{7,6},{8,9},{9,8},{10,11... | collective-permute-start | bytes 786440 | tf_op jit(solution)/shard_map/ppermute | solution.py:29
  49.5 4.3 %collective-permute-start.23 = (bf16[4,128,256]{2,1,0:T(8,128)(2,1)S(1)}, bf16[4,128,256]{2,1,0:T(8,128)(2,1)S(1)}, u32[]{:S(2)}, u32[]{:S(2)}) collective-permute-start(bf16[4,128,256]{2,1,0:T(8,128)(2,1)S(1)} %shard_map.86), channel_id=1, source_target_pairs={{0,1},{1,0},{2,3},{3,2},{4,5},{5,4},{6,7},{7,6},{8,9},{9,8},{10,11... | collective-permute-start | bytes 786440 | tf_op jit(solution)/shard_map/ppermute | solution.py:29
  49.9 6.4 %collective-permute-start.14 = (bf16[128,256]{1,0:T(8,128)(2,1)S(1)}, bf16[128,256]{1,0:T(8,128)(2,1)S(1)}, u32[]{:S(2)}, u32[]{:S(2)}) collective-permute-start(bf16[128,256]{1,0:T(8,128)(2,1)S(1)} %get-tuple-element.66), channel_id=1, source_target_pairs={{0,8},{8,0},{16,24},{24,16},{1,9},{9,1},{17,25},{25,17},{2,10},{10... | collective-permute-start | bytes 196616 | tf_op jit(solution)/shard_map/ppermute | solution.py:29
  51.7 5.7 %collective-permute-start.15 = (bf16[128,256]{1,0:T(8,128)(2,1)S(1)}, bf16[128,256]{1,0:T(8,128)(2,1)S(1)}, u32[]{:S(2)}, u32[]{:S(2)}) collective-permute-start(bf16[128,256]{1,0:T(8,128)(2,1)S(1)} %get-tuple-element.67), channel_id=1, source_target_pairs={{0,16},{8,24},{16,0},{24,8},{1,17},{9,25},{17,1},{25,9},{2,18},{10... | collective-permute-start | bytes 196616 | tf_op jit(solution)/shard_map/ppermute | solution.py:29
  52.7 5.6 %collective-permute-start.16 = (bf16[128,256]{1,0:T(8,128)(2,1)S(1)}, bf16[128,256]{1,0:T(8,128)(2,1)S(1)}, u32[]{:S(2)}, u32[]{:S(2)}) collective-permute-start(bf16[128,256]{1,0:T(8,128)(2,1)S(1)} %get-tuple-element.68), channel_id=1, source_target_pairs={{0,24},{8,16},{16,8},{24,0},{1,25},{9,17},{17,9},{25,1},{2,26},{10... | collective-permute-start | bytes 196616 | tf_op jit(solution)/shard_map/ppermute | solution.py:29
  53.9 4.8 %collective-permute-start.24 = (bf16[128,256]{1,0:T(8,128)(2,1)S(1)}, bf16[128,256]{1,0:T(8,128)(2,1)S(1)}, u32[]{:S(2)}, u32[]{:S(2)}) collective-permute-start(bf16[128,256]{1,0:T(8,128)(2,1)S(1)} %get-tuple-element.78), channel_id=1, source_target_pairs={{0,8},{8,0},{16,24},{24,16},{1,9},{9,1},{17,25},{25,17},{2,10},{10... | collective-permute-start | bytes 196616 | tf_op jit(solution)/shard_map/ppermute | solution.py:29
  55.4 4.9 %collective-permute-start.25 = (bf16[128,256]{1,0:T(8,128)(2,1)S(1)}, bf16[128,256]{1,0:T(8,128)(2,1)S(1)}, u32[]{:S(2)}, u32[]{:S(2)}) collective-permute-start(bf16[128,256]{1,0:T(8,128)(2,1)S(1)} %get-tuple-element.79), channel_id=1, source_target_pairs={{0,16},{8,24},{16,0},{24,8},{1,17},{9,25},{17,1},{25,9},{2,18},{10... | collective-permute-start | bytes 196616 | tf_op jit(solution)/shard_map/ppermute | solution.py:29
  56.3 5.2 %collective-permute-start.26 = (bf16[128,256]{1,0:T(8,128)(2,1)S(1)}, bf16[128,256]{1,0:T(8,128)(2,1)S(1)}, u32[]{:S(2)}, u32[]{:S(2)}) collective-permute-start(bf16[128,256]{1,0:T(8,128)(2,1)S(1)} %get-tuple-element.80), channel_id=1, source_target_pairs={{0,24},{8,16},{16,8},{24,0},{1,25},{9,17},{17,9},{25,1},{2,26},{10... | collective-permute-start | bytes 196616 | tf_op jit(solution)/shard_map/ppermute | solution.py:29

commit v2 on v1

--- a/solution.py
+++ b/solution.py
@@ -356,15 +356,15 @@
             spaces=[HBM] * len(arrays),
         )
 
-    tokens_in, cot_in, momentum_in = loaded(tokens, cotangent, momentum)
+    tokens_in, cot_in, momentum_in, ids_in = loaded(tokens, cotangent, momentum, row_ids)
     x0, own_gram = call(
         front_kernel,
         [tokens_in, peer_tokens, cot_in, peer_cot, momentum_in],
         [((half_rows, hidden), bf16), ((hidden // 2, hidden + hidden // 2), bf16)],
     )
     peer_gram = swapped(own_gram)
-    weight_in, ids_in = loaded(weight, row_ids)
-    peer_ids = swapped(row_ids)
+    (weight_in,) = loaded(weight)
+    peer_ids = swapped(ids_in)
 
     which, *token_cuts = call(
         functools.partial(choose_kernel, hosts),

time: 62.3 us -> 62.9 us (level)
  starting transfers between devices: 30.2 us -> 32.7 us
  waiting for transfers between devices: 21.7 us -> 19.8 us
    ppermute x27, starting transfers between devices: 30.2 us -> 32.7 us  [shifted(): return lax.ppermute(shard, axis, [(i, i ^ k * stride) for i in range(size)])]
    ppermute x27, waiting for transfers between devices: 21.7 us -> 19.8 us  [shifted(): return lax.ppermute(shard, axis, [(i, i ^ k * stride) for i in range(size)])]
  transfers between devices with their start and end apart: 27 -> 27, of which waited for: 11 -> 12; matrix products, arithmetic and copies ran while one was open for 0% -> 0% of each run, Pallas kernels for 9% -> 9%
where the time goes in v2:
time: 62.9 us; the launch traced here: 62.7 us
  starting transfers between devices  32.7 us (52%)
  waiting for transfers between devices  19.8 us (31%)
  Pallas kernels  10 us (16%)
    ppermute x27, starting transfers between devices, shifted(): return lax.ppermute(shard, axis, [(i, i ^ k * stride) for i in range(size)])  32.7 us
    ppermute x27, waiting for transfers between devices, shifted(): return lax.ppermute(shard, axis, [(i, i ^ k * stride) for i in range(size)])  19.8 us
    pallas_call x16, Pallas kernels, call(): pl.pallas_call(kernel, out_shape=[made[where](*out) for where, out in zip...  10 us
  transfers between devices with their start and end apart: 27, of which 12 were waited for; matrix products, arithmetic and copies ran while one was open for 0% of the time, Pallas kernels for 9%

profile of v2, /device:TPU:0, one launch (start us, length us, event | category | flops | bytes accessed | tf_op | source)
XLA Modules:
  0.0 62.7 jit_solution(17735559129684834543)
XLA Ops:
  0.0 0.5 collective-permute-start
  0.5 0.0 collective-permute-start.5
  0.5 1.5 %shard_map.73 = (bf16[128,2048]{1,0:T(8,128)(2,1)S(1)}, bf16[128,512]{1,0:T(8,128)(2,1)S(1)}, bf16[1024,512]{1,0:T(8,128)(2,1)S(1)}, s32[1,128]{1,0:T(1,128)S(1)}) custom-call(bf16[128,2048]{1,0:T(8,128)(2,1)} %refs_0_.1, bf16[128,512]{1,0:T(8,128)(2,1)} %refs_1_.1, bf16[1024,512]{1,0:T(8,128)(2,1)} %bitcast.2, s32[1,128]{1,0:T(1,128)} %refs_3_.1), custom_call_target="tpu_custom_call" | custom-call | tf_op jit(solution)/shard_map/pallas_call | solution.py:290
  2.0 0.4 collective-permute-done.5.peer_cot_ref
  2.4 1.4 %shard_map.75 = (bf16[1024,512]{1,0:T(8,128)(2,1)S(1)}, bf16[256,768]{1,0:T(8,128)(2,1)S(1)}) custom-call(bf16[128,2048]{1,0:T(8,128)(2,1)S(1)} %get-tuple-element.42.own_ref, bf16[128,2048]{1,0:T(8,128)(2,1)S(1)} %collective-permute-done.peer_ref, bf16[128,512]{1,0:T(8,128)(2,1)S(1)} %get-tuple-element.49.cot_ref, ...), custom_call_target="tpu_custom_call" | custom-call | tf_op jit(solution)/shard_map/pallas_call | solution.py:290
  3.8 0.4 collective-permute-start.6
  4.2 1.2 %shard_map.76.weight_ref = bf16[1024,512]{1,0:T(8,128)(2,1)S(1)} custom-call(bf16[1024,512]{1,0:T(8,128)(2,1)} %bitcast.3), custom_call_target="tpu_custom_call" | custom-call | tf_op jit(solution)/shard_map/pallas_call | solution.py:290
  5.5 0.1 collective-permute-done.6.peer_ref
  5.6 2.1 %shard_map.77 = (bf16[512,512]{1,0:T(8,128)(2,1)S(1)}, f32[8,128]{1,0:T(8,128)S(1)}, bf16[256,256]{1,0:T(8,128)(2,1)S(1)}) custom-call(bf16[256,768]{1,0:T(8,128)(2,1)S(1)} %get-tuple-element.51.own_ref, bf16[256,768]{1,0:T(8,128)(2,1)S(1)} %collective-permute-done.6.peer_ref, bf16[1024,512]{1,0:T(8,128)(2,1)S(1)} %get-tuple-element.52.x0_ref, ...), custom_call_target="tpu_custom_call" | custom-call | tf_op jit(solution)/shard_map/pallas_call | solution.py:290
  7.7 0.4 shard_map.78
  8.1 3.0 %collective-permute-start.7 = (bf16[256,256]{1,0:T(8,128)(2,1)S(1)}, bf16[256,256]{1,0:T(8,128)(2,1)S(1)}, u32[]{:S(2)}, u32[]{:S(2)}) collective-permute-start(bf16[256,256]{1,0:T(8,128)(2,1)S(1)} %get-tuple-element.56), channel_id=1, source_target_pairs={{0,8},{8,0},{16,24},{24,16},{1,9},{9,1},{17,25},{25,17},{2,10},{10... | collective-permute-start | bytes 393224 | tf_op jit(solution)/shard_map/ppermute | solution.py:29
  11.1 1.5 %collective-permute-start.8 = (bf16[256,256]{1,0:T(8,128)(2,1)S(1)}, bf16[256,256]{1,0:T(8,128)(2,1)S(1)}, u32[]{:S(2)}, u32[]{:S(2)}) collective-permute-start(bf16[256,256]{1,0:T(8,128)(2,1)S(1)} %get-tuple-element.57), channel_id=1, source_target_pairs={{0,16},{8,24},{16,0},{24,8},{1,17},{9,25},{17,1},{25,9},{2,18},{10... | collective-permute-start | bytes 393224 | tf_op jit(solution)/shard_map/ppermute | solution.py:29
  12.6 0.1 collective-permute-start.9
  12.6 1.1 %collective-permute-done.1.peer_ids_ref = s32[1,128]{1,0:T(1,128)S(1)} collective-permute-done((s32[1,128]{1,0:T(1,128)S(1)}, s32[1,128]{1,0:T(1,128)S(1)}, u32[]{:S(2)}, u32[]{:S(2)}) %collective-permute-start.1) | collective-permute-done | bytes 544 | tf_op jit(solution)/shard_map/ppermute | solution.py:29
  13.7 0.9 %shard_map.74 = (s32[8]{0:T(128)S(4)}, bf16[2,128,256]{2,1,0:T(8,128)(2,1)S(1)}, bf16[2,128,256]{2,1,0:T(8,128)(2,1)S(1)}, bf16[2,128,256]{2,1,0:T(8,128)(2,1)S(1)}, bf16[2,128,256]{2,1,0:T(8,128)(2,1)S(1)}) custom-call(s32[4,4]{1,0:T(4,128)S(1)} %copy-done, s32[4,8]{1,0:T(4,128)S(1)} %copy-done.1, bf16[128,2048]{1,0:T(8,128)(2,1)S(1)} %get-tuple-element.42.own_ref, ...), custom_call_target="tpu_custom_call" | custom-call | tf_op jit(solution)/shard_map/pallas_call | solution.py:290
  14.7 0.9 %collective-permute-start.2 = (bf16[2,128,256]{2,1,0:T(8,128)(2,1)S(1)}, bf16[2,128,256]{2,1,0:T(8,128)(2,1)S(1)}, u32[]{:S(2)}, u32[]{:S(2)}) collective-permute-start(bf16[2,128,256]{2,1,0:T(8,128)(2,1)S(1)} %get-tuple-element.46), channel_id=1, source_target_pairs={{0,8},{8,0},{16,24},{24,16},{1,9},{9,1},{17,25},{25,17},{2,10},{10... | collective-permute-start | bytes 393224 | tf_op jit(solution)/shard_map/ppermute | solution.py:29
  15.6 0.5 shard_map.83
  16.1 1.3 %collective-permute-start.17 = (bf16[256,256]{1,0:T(8,128)(2,1)S(1)}, bf16[256,256]{1,0:T(8,128)(2,1)S(1)}, u32[]{:S(2)}, u32[]{:S(2)}) collective-permute-start(bf16[256,256]{1,0:T(8,128)(2,1)S(1)} %get-tuple-element.68), channel_id=1, source_target_pairs={{0,8},{8,0},{16,24},{24,16},{1,9},{9,1},{17,25},{25,17},{2,10},{10... | collective-permute-start | bytes 393224 | tf_op jit(solution)/shard_map/ppermute | solution.py:29
  17.4 0.0 collective-permute-done.7.refs_1_
  17.4 0.9 %collective-permute-start.18 = (bf16[256,256]{1,0:T(8,128)(2,1)S(1)}, bf16[256,256]{1,0:T(8,128)(2,1)S(1)}, u32[]{:S(2)}, u32[]{:S(2)}) collective-permute-start(bf16[256,256]{1,0:T(8,128)(2,1)S(1)} %get-tuple-element.69), channel_id=1, source_target_pairs={{0,16},{8,24},{16,0},{24,8},{1,17},{9,25},{17,1},{25,9},{2,18},{10... | collective-permute-start | bytes 393224 | tf_op jit(solution)/shard_map/ppermute | solution.py:29
  18.2 0.0 collective-permute-done.8.refs_2_
  18.2 2.0 %collective-permute-start.19 = (bf16[256,256]{1,0:T(8,128)(2,1)S(1)}, bf16[256,256]{1,0:T(8,128)(2,1)S(1)}, u32[]{:S(2)}, u32[]{:S(2)}) collective-permute-start(bf16[256,256]{1,0:T(8,128)(2,1)S(1)} %get-tuple-element.70), channel_id=1, source_target_pairs={{0,24},{8,16},{16,8},{24,0},{1,25},{9,17},{17,9},{25,1},{2,26},{10... | collective-permute-start | bytes 393224 | tf_op jit(solution)/shard_map/ppermute | solution.py:29
  20.2 0.9 %collective-permute-start.3 = (bf16[2,128,256]{2,1,0:T(8,128)(2,1)S(1)}, bf16[2,128,256]{2,1,0:T(8,128)(2,1)S(1)}, u32[]{:S(2)}, u32[]{:S(2)}) collective-permute-start(bf16[2,128,256]{2,1,0:T(8,128)(2,1)S(1)} %get-tuple-element.47), channel_id=1, source_target_pairs={{0,16},{8,24},{16,0},{24,8},{1,17},{9,25},{17,1},{25,9},{2,18},{10... | collective-permute-start | bytes 393224 | tf_op jit(solution)/shard_map/ppermute | solution.py:29
  21.2 0.1 shard_map.79
  21.2 0.5 collective-permute-done.2.refs_1_
  21.8 2.1 %collective-permute-start.4 = (bf16[2,128,256]{2,1,0:T(8,128)(2,1)S(1)}, bf16[2,128,256]{2,1,0:T(8,128)(2,1)S(1)}, u32[]{:S(2)}, u32[]{:S(2)}) collective-permute-start(bf16[2,128,256]{2,1,0:T(8,128)(2,1)S(1)} %get-tuple-element.48), channel_id=1, source_target_pairs={{0,24},{8,16},{16,8},{24,0},{1,25},{9,17},{17,9},{25,1},{2,26},{10... | collective-permute-start | bytes 393224 | tf_op jit(solution)/shard_map/ppermute | solution.py:29
  23.9 0.7 %collective-permute-done.17.refs_1_ = bf16[256,256]{1,0:T(8,128)(2,1)S(1)} collective-permute-done((bf16[256,256]{1,0:T(8,128)(2,1)S(1)}, bf16[256,256]{1,0:T(8,128)(2,1)S(1)}, u32[]{:S(2)}, u32[]{:S(2)}) %collective-permute-start.17) | collective-permute-done | bytes 131104 | tf_op jit(solution)/shard_map/ppermute | solution.py:29
  24.6 1.6 %collective-permute-start.10 = (bf16[256,256]{1,0:T(8,128)(2,1)S(1)}, bf16[256,256]{1,0:T(8,128)(2,1)S(1)}, u32[]{:S(2)}, u32[]{:S(2)}) collective-permute-start(bf16[256,256]{1,0:T(8,128)(2,1)S(1)} %get-tuple-element.60), channel_id=1, source_target_pairs={{0,2},{1,3},{2,0},{3,1},{4,6},{5,7},{6,4},{7,5},{8,10},{9,11},{10,... | collective-permute-start | bytes 393224 | tf_op jit(solution)/shard_map/ppermute | solution.py:29
  26.1 0.0 collective-permute-done.18.refs_2_
  26.1 2.6 %collective-permute-start.11 = (bf16[256,256]{1,0:T(8,128)(2,1)S(1)}, bf16[256,256]{1,0:T(8,128)(2,1)S(1)}, u32[]{:S(2)}, u32[]{:S(2)}) collective-permute-start(bf16[256,256]{1,0:T(8,128)(2,1)S(1)} %get-tuple-element.61), channel_id=1, source_target_pairs={{0,4},{1,5},{2,6},{3,7},{4,0},{5,1},{6,2},{7,3},{8,12},{9,13},{10,... | collective-permute-start | bytes 393224 | tf_op jit(solution)/shard_map/ppermute | solution.py:29
  28.7 0.0 collective-permute-done.19.refs_3_
  28.7 3.2 %collective-permute-start.12 = (bf16[256,256]{1,0:T(8,128)(2,1)S(1)}, bf16[256,256]{1,0:T(8,128)(2,1)S(1)}, u32[]{:S(2)}, u32[]{:S(2)}) collective-permute-start(bf16[256,256]{1,0:T(8,128)(2,1)S(1)} %get-tuple-element.62), channel_id=1, source_target_pairs={{0,6},{1,7},{2,4},{3,5},{4,2},{5,3},{6,0},{7,1},{8,14},{9,15},{10,... | collective-permute-start | bytes 393224 | tf_op jit(solution)/shard_map/ppermute | solution.py:29
  32.0 0.1 shard_map.84
  32.0 0.0 collective-permute-done.3.refs_2_
  32.0 0.5 collective-permute-start.20
  32.6 0.0 collective-permute-done.4.refs_3_
  32.6 2.6 %collective-permute-start.21 = (bf16[256,256]{1,0:T(8,128)(2,1)S(1)}, bf16[256,256]{1,0:T(8,128)(2,1)S(1)}, u32[]{:S(2)}, u32[]{:S(2)}) collective-permute-start(bf16[256,256]{1,0:T(8,128)(2,1)S(1)} %get-tuple-element.73), channel_id=1, source_target_pairs={{0,4},{1,5},{2,6},{3,7},{4,0},{5,1},{6,2},{7,3},{8,12},{9,13},{10,... | collective-permute-start | bytes 393224 | tf_op jit(solution)/shard_map/ppermute | solution.py:29
  35.2 0.0 collective-permute-done.10.refs_5_
  35.2 1.3 %collective-permute-start.22 = (bf16[256,256]{1,0:T(8,128)(2,1)S(1)}, bf16[256,256]{1,0:T(8,128)(2,1)S(1)}, u32[]{:S(2)}, u32[]{:S(2)}) collective-permute-start(bf16[256,256]{1,0:T(8,128)(2,1)S(1)} %get-tuple-element.74), channel_id=1, source_target_pairs={{0,6},{1,7},{2,4},{3,5},{4,2},{5,3},{6,0},{7,1},{8,14},{9,15},{10,... | collective-permute-start | bytes 393224 | tf_op jit(solution)/shard_map/ppermute | solution.py:29
  36.5 1.2 %collective-permute-done.11.refs_6_ = bf16[256,256]{1,0:T(8,128)(2,1)S(1)} collective-permute-done((bf16[256,256]{1,0:T(8,128)(2,1)S(1)}, bf16[256,256]{1,0:T(8,128)(2,1)S(1)}, u32[]{:S(2)}, u32[]{:S(2)}) %collective-permute-start.11) | collective-permute-done | bytes 131104 | tf_op jit(solution)/shard_map/ppermute | solution.py:29
  37.7 0.8 %collective-permute-done.12.refs_7_ = bf16[256,256]{1,0:T(8,128)(2,1)S(1)} collective-permute-done((bf16[256,256]{1,0:T(8,128)(2,1)S(1)}, bf16[256,256]{1,0:T(8,128)(2,1)S(1)}, u32[]{:S(2)}, u32[]{:S(2)}) %collective-permute-start.12) | collective-permute-done | bytes 131104 | tf_op jit(solution)/shard_map/ppermute | solution.py:29
  38.6 0.3 shard_map.81
  38.8 0.1 collective-permute-start.13
  38.9 0.3 collective-permute-done.20.refs_5_
  39.2 10.2 %collective-permute-done.21.refs_6_ = bf16[256,256]{1,0:T(8,128)(2,1)S(1)} collective-permute-done((bf16[256,256]{1,0:T(8,128)(2,1)S(1)}, bf16[256,256]{1,0:T(8,128)(2,1)S(1)}, u32[]{:S(2)}, u32[]{:S(2)}) %collective-permute-start.21) | collective-permute-done | bytes 131104 | tf_op jit(solution)/shard_map/ppermute | solution.py:29
  49.4 0.0 collective-permute-done.22.refs_7_
  49.4 0.3 shard_map.86
  49.7 0.1 collective-permute-start.23
  49.8 0.3 shard_map.80.keep_ref
  50.0 0.0 collective-permute-done.13.other_ref
  50.1 1.1 %collective-permute-start.14 = (bf16[128,256]{1,0:T(8,128)(2,1)S(1)}, bf16[128,256]{1,0:T(8,128)(2,1)S(1)}, u32[]{:S(2)}, u32[]{:S(2)}) collective-permute-start(bf16[128,256]{1,0:T(8,128)(2,1)S(1)} %get-tuple-element.64), channel_id=1, source_target_pairs={{0,8},{8,0},{16,24},{24,16},{1,9},{9,1},{17,25},{25,17},{2,10},{10... | collective-permute-start | bytes 196616 | tf_op jit(solution)/shard_map/ppermute | solution.py:29
  51.2 0.3 shard_map.85.keep_ref
  51.4 1.8 %collective-permute-start.15 = (bf16[128,256]{1,0:T(8,128)(2,1)S(1)}, bf16[128,256]{1,0:T(8,128)(2,1)S(1)}, u32[]{:S(2)}, u32[]{:S(2)}) collective-permute-start(bf16[128,256]{1,0:T(8,128)(2,1)S(1)} %get-tuple-element.65), channel_id=1, source_target_pairs={{0,16},{8,24},{16,0},{24,8},{1,17},{9,25},{17,1},{25,9},{2,18},{10... | collective-permute-start | bytes 196616 | tf_op jit(solution)/shard_map/ppermute | solution.py:29
  53.2 0.8 %collective-permute-start.16 = (bf16[128,256]{1,0:T(8,128)(2,1)S(1)}, bf16[128,256]{1,0:T(8,128)(2,1)S(1)}, u32[]{:S(2)}, u32[]{:S(2)}) collective-permute-start(bf16[128,256]{1,0:T(8,128)(2,1)S(1)} %get-tuple-element.66), channel_id=1, source_target_pairs={{0,24},{8,16},{16,8},{24,0},{1,25},{9,17},{17,9},{25,1},{2,26},{10... | collective-permute-start | bytes 196616 | tf_op jit(solution)/shard_map/ppermute | solution.py:29
  54.0 0.0 collective-permute-done.23.other_ref
  54.0 1.1 %collective-permute-start.24 = (bf16[128,256]{1,0:T(8,128)(2,1)S(1)}, bf16[128,256]{1,0:T(8,128)(2,1)S(1)}, u32[]{:S(2)}, u32[]{:S(2)}) collective-permute-start(bf16[128,256]{1,0:T(8,128)(2,1)S(1)} %get-tuple-element.76), channel_id=1, source_target_pairs={{0,8},{8,0},{16,24},{24,16},{1,9},{9,1},{17,25},{25,17},{2,10},{10... | collective-permute-start | bytes 196616 | tf_op jit(solution)/shard_map/ppermute | solution.py:29
  55.1 1.7 %collective-permute-start.25 = (bf16[128,256]{1,0:T(8,128)(2,1)S(1)}, bf16[128,256]{1,0:T(8,128)(2,1)S(1)}, u32[]{:S(2)}, u32[]{:S(2)}) collective-permute-start(bf16[128,256]{1,0:T(8,128)(2,1)S(1)} %get-tuple-element.77), channel_id=1, source_target_pairs={{0,16},{8,24},{16,0},{24,8},{1,17},{9,25},{17,1},{25,9},{2,18},{10... | collective-permute-start | bytes 196616 | tf_op jit(solution)/shard_map/ppermute | solution.py:29
  56.8 0.0 collective-permute-done.14.refs_1_
  56.8 0.8 %collective-permute-start.26 = (bf16[128,256]{1,0:T(8,128)(2,1)S(1)}, bf16[128,256]{1,0:T(8,128)(2,1)S(1)}, u32[]{:S(2)}, u32[]{:S(2)}) collective-permute-start(bf16[128,256]{1,0:T(8,128)(2,1)S(1)} %get-tuple-element.78), channel_id=1, source_target_pairs={{0,24},{8,16},{16,8},{24,0},{1,25},{9,17},{17,9},{25,1},{2,26},{10... | collective-permute-start | bytes 196616 | tf_op jit(solution)/shard_map/ppermute | solution.py:29
  57.6 1.3 %collective-permute-done.16.refs_3_ = bf16[128,256]{1,0:T(8,128)(2,1)S(1)} collective-permute-done((bf16[128,256]{1,0:T(8,128)(2,1)S(1)}, bf16[128,256]{1,0:T(8,128)(2,1)S(1)}, u32[]{:S(2)}, u32[]{:S(2)}) %collective-permute-start.16) | collective-permute-done | bytes 65568 | tf_op jit(solution)/shard_map/ppermute | solution.py:29
  59.0 0.0 collective-permute-done.24.refs_5_
  59.0 0.8 %collective-permute-done.25.refs_6_ = bf16[128,256]{1,0:T(8,128)(2,1)S(1)} collective-permute-done((bf16[128,256]{1,0:T(8,128)(2,1)S(1)}, bf16[128,256]{1,0:T(8,128)(2,1)S(1)}, u32[]{:S(2)}, u32[]{:S(2)}) %collective-permute-start.25) | collective-permute-done | bytes 65568 | tf_op jit(solution)/shard_map/ppermute | solution.py:29
  59.7 2.3 %collective-permute-done.26.refs_7_ = bf16[128,256]{1,0:T(8,128)(2,1)S(1)} collective-permute-done((bf16[128,256]{1,0:T(8,128)(2,1)S(1)}, bf16[128,256]{1,0:T(8,128)(2,1)S(1)}, u32[]{:S(2)}, u32[]{:S(2)}) %collective-permute-start.26) | collective-permute-done | bytes 65568 | tf_op jit(solution)/shard_map/ppermute | solution.py:29
  62.0 0.7 %shard_map.88 = bf16[128,512]{1,0:T(8,128)(2,1)} custom-call(bf16[128,256]{1,0:T(8,128)(2,1)S(1)} %get-tuple-element.63.refs_0_, bf16[128,256]{1,0:T(8,128)(2,1)S(1)} %collective-permute-done.14.refs_1_, bf16[128,256]{1,0:T(8,128)(2,1)S(1)} %collective-permute-done.15.refs_2_, bf16[128,256]{1,0:T(8,128)(2,1)S(1)} %collective-permute-done.16.refs_3_, ...), custom_call_target="tpu_custom_call" | custom-call | tf_op jit(solution)/shard_map/pallas_call | solution.py:290
  (10 shorter events, 0.1 us)
Async XLA Ops:
  0.0 2.4 %collective-permute-start = (bf16[128,2048]{1,0:T(8,128)(2,1)}, bf16[128,2048]{1,0:T(8,128)(2,1)S(1)}, u32[]{:S(2)}, u32[]{:S(2)}) collective-permute-start(bf16[128,2048]{1,0:T(8,128)(2,1)} %refs_0_.1), channel_id=1, source_target_pairs={{0,1},{1,0},{2,3},{3,2},{4,5},{5,4},{6,7},{7,6},{8,9},{9,8},{10,11... | collective-permute-start | bytes 1572872 | tf_op jit(solution)/shard_map/ppermute | solution.py:29
  0.5 1.9 %collective-permute-start.5 = (bf16[128,512]{1,0:T(8,128)(2,1)}, bf16[128,512]{1,0:T(8,128)(2,1)S(1)}, u32[]{:S(2)}, u32[]{:S(2)}) collective-permute-start(bf16[128,512]{1,0:T(8,128)(2,1)} %refs_1_.1), channel_id=1, source_target_pairs={{0,1},{1,0},{2,3},{3,2},{4,5},{5,4},{6,7},{7,6},{8,9},{9,8},{10,11... | collective-permute-start | bytes 393224 | tf_op jit(solution)/shard_map/ppermute | solution.py:29
  3.8 1.8 %collective-permute-start.6 = (bf16[256,768]{1,0:T(8,128)(2,1)S(1)}, bf16[256,768]{1,0:T(8,128)(2,1)S(1)}, u32[]{:S(2)}, u32[]{:S(2)}) collective-permute-start(bf16[256,768]{1,0:T(8,128)(2,1)S(1)} %get-tuple-element.51.own_ref), channel_id=1, source_target_pairs={{0,1},{1,0},{2,3},{3,2},{4,5},{5,4},{6,7},{7,6},{8,9},{9,8},{10,11... | collective-permute-start | bytes 1179656 | tf_op jit(solution)/shard_map/ppermute | solution.py:29
  8.1 9.2 %collective-permute-start.7 = (bf16[256,256]{1,0:T(8,128)(2,1)S(1)}, bf16[256,256]{1,0:T(8,128)(2,1)S(1)}, u32[]{:S(2)}, u32[]{:S(2)}) collective-permute-start(bf16[256,256]{1,0:T(8,128)(2,1)S(1)} %get-tuple-element.56), channel_id=1, source_target_pairs={{0,8},{8,0},{16,24},{24,16},{1,9},{9,1},{17,25},{25,17},{2,10},{10... | collective-permute-start | bytes 393224 | tf_op jit(solution)/shard_map/ppermute | solution.py:29
  11.1 2.7 %copy-start.1 = (s32[4,8]{1,0:T(4,128)S(1)}, s32[4,8]{1,0:T(4,128)}, u32[]{:S(2)}) copy-start(s32[4,8]{1,0:T(4,128)} %new_ref.1) | copy-start | bytes 388
  11.1 2.7 %copy-start = (s32[4,4]{1,0:T(4,128)S(1)}, s32[4,4]{1,0:T(4,128)}, u32[]{:S(2)}) copy-start(s32[4,4]{1,0:T(4,128)} %old_ref.1) | copy-start | bytes 196
  11.1 7.1 %collective-permute-start.8 = (bf16[256,256]{1,0:T(8,128)(2,1)S(1)}, bf16[256,256]{1,0:T(8,128)(2,1)S(1)}, u32[]{:S(2)}, u32[]{:S(2)}) collective-permute-start(bf16[256,256]{1,0:T(8,128)(2,1)S(1)} %get-tuple-element.57), channel_id=1, source_target_pairs={{0,16},{8,24},{16,0},{24,8},{1,17},{9,25},{17,1},{25,9},{2,18},{10... | collective-permute-start | bytes 393224 | tf_op jit(solution)/shard_map/ppermute | solution.py:29
  12.6 1.2 %collective-permute-start.1 = (s32[1,128]{1,0:T(1,128)S(1)}, s32[1,128]{1,0:T(1,128)S(1)}, u32[]{:S(2)}, u32[]{:S(2)}) collective-permute-start(s32[1,128]{1,0:T(1,128)S(1)} %get-tuple-element.43.ids_ref), channel_id=1, source_target_pairs={{0,1},{1,0},{2,3},{3,2},{4,5},{5,4},{6,7},{7,6},{8,9},{9,8},{10,11... | collective-permute-start | bytes 1544 | tf_op jit(solution)/shard_map/ppermute | solution.py:29
  12.6 7.6 %collective-permute-start.9 = (bf16[256,256]{1,0:T(8,128)(2,1)S(1)}, bf16[256,256]{1,0:T(8,128)(2,1)S(1)}, u32[]{:S(2)}, u32[]{:S(2)}) collective-permute-start(bf16[256,256]{1,0:T(8,128)(2,1)S(1)} %get-tuple-element.58), channel_id=1, source_target_pairs={{0,24},{8,16},{16,8},{24,0},{1,25},{9,17},{17,9},{25,1},{2,26},{10... | collective-permute-start | bytes 393224 | tf_op jit(solution)/shard_map/ppermute | solution.py:29
  14.7 7.1 %collective-permute-start.2 = (bf16[2,128,256]{2,1,0:T(8,128)(2,1)S(1)}, bf16[2,128,256]{2,1,0:T(8,128)(2,1)S(1)}, u32[]{:S(2)}, u32[]{:S(2)}) collective-permute-start(bf16[2,128,256]{2,1,0:T(8,128)(2,1)S(1)} %get-tuple-element.46), channel_id=1, source_target_pairs={{0,8},{8,0},{16,24},{24,16},{1,9},{9,1},{17,25},{25,17},{2,10},{10... | collective-permute-start | bytes 393224 | tf_op jit(solution)/shard_map/ppermute | solution.py:29
  16.1 8.5 %collective-permute-start.17 = (bf16[256,256]{1,0:T(8,128)(2,1)S(1)}, bf16[256,256]{1,0:T(8,128)(2,1)S(1)}, u32[]{:S(2)}, u32[]{:S(2)}) collective-permute-start(bf16[256,256]{1,0:T(8,128)(2,1)S(1)} %get-tuple-element.68), channel_id=1, source_target_pairs={{0,8},{8,0},{16,24},{24,16},{1,9},{9,1},{17,25},{25,17},{2,10},{10... | collective-permute-start | bytes 393224 | tf_op jit(solution)/shard_map/ppermute | solution.py:29
  17.4 8.8 %collective-permute-start.18 = (bf16[256,256]{1,0:T(8,128)(2,1)S(1)}, bf16[256,256]{1,0:T(8,128)(2,1)S(1)}, u32[]{:S(2)}, u32[]{:S(2)}) collective-permute-start(bf16[256,256]{1,0:T(8,128)(2,1)S(1)} %get-tuple-element.69), channel_id=1, source_target_pairs={{0,16},{8,24},{16,0},{24,8},{1,17},{9,25},{17,1},{25,9},{2,18},{10... | collective-permute-start | bytes 393224 | tf_op jit(solution)/shard_map/ppermute | solution.py:29
  18.2 10.5 %collective-permute-start.19 = (bf16[256,256]{1,0:T(8,128)(2,1)S(1)}, bf16[256,256]{1,0:T(8,128)(2,1)S(1)}, u32[]{:S(2)}, u32[]{:S(2)}) collective-permute-start(bf16[256,256]{1,0:T(8,128)(2,1)S(1)} %get-tuple-element.70), channel_id=1, source_target_pairs={{0,24},{8,16},{16,8},{24,0},{1,25},{9,17},{17,9},{25,1},{2,26},{10... | collective-permute-start | bytes 393224 | tf_op jit(solution)/shard_map/ppermute | solution.py:29
  20.2 11.8 %collective-permute-start.3 = (bf16[2,128,256]{2,1,0:T(8,128)(2,1)S(1)}, bf16[2,128,256]{2,1,0:T(8,128)(2,1)S(1)}, u32[]{:S(2)}, u32[]{:S(2)}) collective-permute-start(bf16[2,128,256]{2,1,0:T(8,128)(2,1)S(1)} %get-tuple-element.47), channel_id=1, source_target_pairs={{0,16},{8,24},{16,0},{24,8},{1,17},{9,25},{17,1},{25,9},{2,18},{10... | collective-permute-start | bytes 393224 | tf_op jit(solution)/shard_map/ppermute | solution.py:29
  21.8 10.8 %collective-permute-start.4 = (bf16[2,128,256]{2,1,0:T(8,128)(2,1)S(1)}, bf16[2,128,256]{2,1,0:T(8,128)(2,1)S(1)}, u32[]{:S(2)}, u32[]{:S(2)}) collective-permute-start(bf16[2,128,256]{2,1,0:T(8,128)(2,1)S(1)} %get-tuple-element.48), channel_id=1, source_target_pairs={{0,24},{8,16},{16,8},{24,0},{1,25},{9,17},{17,9},{25,1},{2,26},{10... | collective-permute-start | bytes 393224 | tf_op jit(solution)/shard_map/ppermute | solution.py:29
  24.6 10.6 %collective-permute-start.10 = (bf16[256,256]{1,0:T(8,128)(2,1)S(1)}, bf16[256,256]{1,0:T(8,128)(2,1)S(1)}, u32[]{:S(2)}, u32[]{:S(2)}) collective-permute-start(bf16[256,256]{1,0:T(8,128)(2,1)S(1)} %get-tuple-element.60), channel_id=1, source_target_pairs={{0,2},{1,3},{2,0},{3,1},{4,6},{5,7},{6,4},{7,5},{8,10},{9,11},{10,... | collective-permute-start | bytes 393224 | tf_op jit(solution)/shard_map/ppermute | solution.py:29
  26.1 11.6 %collective-permute-start.11 = (bf16[256,256]{1,0:T(8,128)(2,1)S(1)}, bf16[256,256]{1,0:T(8,128)(2,1)S(1)}, u32[]{:S(2)}, u32[]{:S(2)}) collective-permute-start(bf16[256,256]{1,0:T(8,128)(2,1)S(1)} %get-tuple-element.61), channel_id=1, source_target_pairs={{0,4},{1,5},{2,6},{3,7},{4,0},{5,1},{6,2},{7,3},{8,12},{9,13},{10,... | collective-permute-start | bytes 393224 | tf_op jit(solution)/shard_map/ppermute | solution.py:29
  28.7 9.8 %collective-permute-start.12 = (bf16[256,256]{1,0:T(8,128)(2,1)S(1)}, bf16[256,256]{1,0:T(8,128)(2,1)S(1)}, u32[]{:S(2)}, u32[]{:S(2)}) collective-permute-start(bf16[256,256]{1,0:T(8,128)(2,1)S(1)} %get-tuple-element.62), channel_id=1, source_target_pairs={{0,6},{1,7},{2,4},{3,5},{4,2},{5,3},{6,0},{7,1},{8,14},{9,15},{10,... | collective-permute-start | bytes 393224 | tf_op jit(solution)/shard_map/ppermute | solution.py:29
  32.0 7.1 %collective-permute-start.20 = (bf16[256,256]{1,0:T(8,128)(2,1)S(1)}, bf16[256,256]{1,0:T(8,128)(2,1)S(1)}, u32[]{:S(2)}, u32[]{:S(2)}) collective-permute-start(bf16[256,256]{1,0:T(8,128)(2,1)S(1)} %get-tuple-element.72), channel_id=1, source_target_pairs={{0,2},{1,3},{2,0},{3,1},{4,6},{5,7},{6,4},{7,5},{8,10},{9,11},{10,... | collective-permute-start | bytes 393224 | tf_op jit(solution)/shard_map/ppermute | solution.py:29
  32.6 16.8 %collective-permute-start.21 = (bf16[256,256]{1,0:T(8,128)(2,1)S(1)}, bf16[256,256]{1,0:T(8,128)(2,1)S(1)}, u32[]{:S(2)}, u32[]{:S(2)}) collective-permute-start(bf16[256,256]{1,0:T(8,128)(2,1)S(1)} %get-tuple-element.73), channel_id=1, source_target_pairs={{0,4},{1,5},{2,6},{3,7},{4,0},{5,1},{6,2},{7,3},{8,12},{9,13},{10,... | collective-permute-start | bytes 393224 | tf_op jit(solution)/shard_map/ppermute | solution.py:29
  35.2 14.2 %collective-permute-start.22 = (bf16[256,256]{1,0:T(8,128)(2,1)S(1)}, bf16[256,256]{1,0:T(8,128)(2,1)S(1)}, u32[]{:S(2)}, u32[]{:S(2)}) collective-permute-start(bf16[256,256]{1,0:T(8,128)(2,1)S(1)} %get-tuple-element.74), channel_id=1, source_target_pairs={{0,6},{1,7},{2,4},{3,5},{4,2},{5,3},{6,0},{7,1},{8,14},{9,15},{10,... | collective-permute-start | bytes 393224 | tf_op jit(solution)/shard_map/ppermute | solution.py:29
  38.8 11.2 %collective-permute-start.13 = (bf16[4,128,256]{2,1,0:T(8,128)(2,1)S(1)}, bf16[4,128,256]{2,1,0:T(8,128)(2,1)S(1)}, u32[]{:S(2)}, u32[]{:S(2)}) collective-permute-start(bf16[4,128,256]{2,1,0:T(8,128)(2,1)S(1)} %shard_map.81), channel_id=1, source_target_pairs={{0,1},{1,0},{2,3},{3,2},{4,5},{5,4},{6,7},{7,6},{8,9},{9,8},{10,11... | collective-permute-start | bytes 786440 | tf_op jit(solution)/shard_map/ppermute | solution.py:29
  49.7 4.3 %collective-permute-start.23 = (bf16[4,128,256]{2,1,0:T(8,128)(2,1)S(1)}, bf16[4,128,256]{2,1,0:T(8,128)(2,1)S(1)}, u32[]{:S(2)}, u32[]{:S(2)}) collective-permute-start(bf16[4,128,256]{2,1,0:T(8,128)(2,1)S(1)} %shard_map.86), channel_id=1, source_target_pairs={{0,1},{1,0},{2,3},{3,2},{4,5},{5,4},{6,7},{7,6},{8,9},{9,8},{10,11... | collective-permute-start | bytes 786440 | tf_op jit(solution)/shard_map/ppermute | solution.py:29
  50.1 6.7 %collective-permute-start.14 = (bf16[128,256]{1,0:T(8,128)(2,1)S(1)}, bf16[128,256]{1,0:T(8,128)(2,1)S(1)}, u32[]{:S(2)}, u32[]{:S(2)}) collective-permute-start(bf16[128,256]{1,0:T(8,128)(2,1)S(1)} %get-tuple-element.64), channel_id=1, source_target_pairs={{0,8},{8,0},{16,24},{24,16},{1,9},{9,1},{17,25},{25,17},{2,10},{10... | collective-permute-start | bytes 196616 | tf_op jit(solution)/shard_map/ppermute | solution.py:29
  51.4 6.2 %collective-permute-start.15 = (bf16[128,256]{1,0:T(8,128)(2,1)S(1)}, bf16[128,256]{1,0:T(8,128)(2,1)S(1)}, u32[]{:S(2)}, u32[]{:S(2)}) collective-permute-start(bf16[128,256]{1,0:T(8,128)(2,1)S(1)} %get-tuple-element.65), channel_id=1, source_target_pairs={{0,16},{8,24},{16,0},{24,8},{1,17},{9,25},{17,1},{25,9},{2,18},{10... | collective-permute-start | bytes 196616 | tf_op jit(solution)/shard_map/ppermute | solution.py:29
  53.2 5.7 %collective-permute-start.16 = (bf16[128,256]{1,0:T(8,128)(2,1)S(1)}, bf16[128,256]{1,0:T(8,128)(2,1)S(1)}, u32[]{:S(2)}, u32[]{:S(2)}) collective-permute-start(bf16[128,256]{1,0:T(8,128)(2,1)S(1)} %get-tuple-element.66), channel_id=1, source_target_pairs={{0,24},{8,16},{16,8},{24,0},{1,25},{9,17},{17,9},{25,1},{2,26},{10... | collective-permute-start | bytes 196616 | tf_op jit(solution)/shard_map/ppermute | solution.py:29
  54.0 4.9 %collective-permute-start.24 = (bf16[128,256]{1,0:T(8,128)(2,1)S(1)}, bf16[128,256]{1,0:T(8,128)(2,1)S(1)}, u32[]{:S(2)}, u32[]{:S(2)}) collective-permute-start(bf16[128,256]{1,0:T(8,128)(2,1)S(1)} %get-tuple-element.76), channel_id=1, source_target_pairs={{0,8},{8,0},{16,24},{24,16},{1,9},{9,1},{17,25},{25,17},{2,10},{10... | collective-permute-start | bytes 196616 | tf_op jit(solution)/shard_map/ppermute | solution.py:29
  55.1 4.6 %collective-permute-start.25 = (bf16[128,256]{1,0:T(8,128)(2,1)S(1)}, bf16[128,256]{1,0:T(8,128)(2,1)S(1)}, u32[]{:S(2)}, u32[]{:S(2)}) collective-permute-start(bf16[128,256]{1,0:T(8,128)(2,1)S(1)} %get-tuple-element.77), channel_id=1, source_target_pairs={{0,16},{8,24},{16,0},{24,8},{1,17},{9,25},{17,1},{25,9},{2,18},{10... | collective-permute-start | bytes 196616 | tf_op jit(solution)/shard_map/ppermute | solution.py:29
  56.8 5.2 %collective-permute-start.26 = (bf16[128,256]{1,0:T(8,128)(2,1)S(1)}, bf16[128,256]{1,0:T(8,128)(2,1)S(1)}, u32[]{:S(2)}, u32[]{:S(2)}) collective-permute-start(bf16[128,256]{1,0:T(8,128)(2,1)S(1)} %get-tuple-element.78), channel_id=1, source_target_pairs={{0,24},{8,16},{16,8},{24,0},{1,25},{9,17},{17,9},{25,1},{2,26},{10... | collective-permute-start | bytes 196616 | tf_op jit(solution)/shard_map/ppermute | solution.py:29
